TPU v7x, 32 devices: a whole 2x2x4 slice. The times are simulated.
32 devices in a mesh: row: 8 (over z, x), col: 4 (over y, core).
Axes of the slice: x: 2, y: 2, z: 4, core: 2. Of those that a mesh axis runs over, the one named last changes fastest.
Arguments:
- subspace: bfloat16 [256, 32768], P('col', 'row'), may hold values from -400 to 400
- onsite: float32 [32768], P('row'), may hold values from -1.5 to 1.5
- blocks: bfloat16 [20, 256, 128, 128], P(None, 'row'), may hold values from -0.125 to 0.125
- cols: int32 [256, 20], replicated, may hold values from 0 to 255, as said below
Outputs:
- basis: float32 [256, 32768], P('col', 'row')
- factor: float32 [256, 256], replicated
Inputs may be any that keep to these rules, and one draw needn't show every extreme that they name: `cols`: the block rows are numbered by device: device r of row holds block rows r * 32 to (r + 1) * 32 - 1. A block row names block rows of its own device or of the devices r + 1, r - 1, r + 2 and r + 4 along row, counted round. The block rows of one device name between 1 and 4 distinct block rows of each of these four devices, and in every draw some device names exactly 4 on each of its four.
All inputs are finite; a program needn't handle non-finite values.
Results may differ from a plain program's by a relative error of at most 0.0044.
Values may be sent and summed in bfloat16 or wider, within the bound.
A program may use at most 128 MiB of HBM per device.

v0:
```python
import functools
import math

import jax
import jax.numpy as jnp
from jax import lax
from jax.experimental import pallas as pl
from jax.experimental.pallas import tpu as pltpu
from jax.sharding import PartitionSpec as P

HALO = 4
FILTER = 4
UNROLL = 4
HALVES = 1
filter_scale = 0.4
f32 = jnp.float32
bf16 = jnp.bfloat16


def shifts_of(rows):
    return (rows // 2, 2, 1, -1)


def index_tables(cols, rows, me, lb):
    sc = cols.shape[1]
    shifts = shifts_of(rows)
    groups = len(shifts)
    own = lax.dynamic_slice_in_dim(cols, me * lb, lb, 0).reshape(-1)
    askers = [
        lax.dynamic_slice_in_dim(cols, lax.rem(me - d + rows, rows) * lb, lb, 0).reshape(-1)
        for d in shifts
    ]
    owners = jnp.stack([lax.rem(me + d + rows, rows) for d in shifts])
    k = jnp.arange(lb, dtype=jnp.int32)
    wanted = own[None, :] - owners[:, None] * lb
    asked = jnp.stack(askers) - me * lb
    rel = jnp.concatenate([wanted, asked], 0)
    hit = jnp.any(rel[:, :, None] == k, axis=1)
    before = (k[:, None] < k[None, :])
    rank = jnp.sum((hit[:, :, None] & before[None]).astype(jnp.int32), axis=1)
    hit_e, rank_e = hit[groups:], rank[groups:]
    g = jnp.arange(groups, dtype=jnp.int32)
    key = jnp.min(jnp.where(hit_e, g[:, None], groups), axis=0)
    ahead = (key[:, None] < key[None, :]) | ((key[:, None] == key[None, :]) & before)
    inv = jnp.sum(ahead.astype(jnp.int32), axis=0)
    perm = jnp.sum(jnp.where(inv[None, :] == k[:, None], k[None, :], 0), axis=1)
    m = jnp.arange(HALO, dtype=jnp.int32)
    pick = hit_e[:, None, :] & (rank_e[:, None, :] == m[:, None])
    exp_n = jnp.sum(jnp.where(pick, k, 0), axis=-1)
    exp_p = jnp.sum(jnp.where(pick, inv, 0), axis=-1)
    slot = lb + HALO * g[:, None] + rank[:groups]
    match = wanted[:, :, None] == k
    far = jnp.sum(jnp.where(match, slot[:, None, :], 0), axis=(0, 2))
    near = own - me * lb
    mine = (near >= 0) & (near < lb)
    near_p = jnp.sum(jnp.where(near[:, None] == k, inv, 0), axis=1)
    pos_n = jnp.where(mine, near, far)
    pos_p = jnp.where(mine, near_p, far)
    return jnp.concatenate(
        [pos_n, pos_p, perm, inv, exp_n.reshape(-1), exp_p.reshape(-1)]
    ).astype(jnp.int32)


def flip(c, bit):
    return c + bit - 2 * bit * lax.rem(c // bit, 2)


def hops_of(parts):
    hops, held, bit = [], [0], parts // 2
    while bit:
        hops += [(bit, m) for m in held]
        held += [m + bit for m in held]
        bit //= 2
    return hops


def slice_of(width, rows):
    return max(8, width // rows)


def filter_kernel(rows, parts, lb, sc, tab, sub, ons, blk, out, gram, bm, *refs):
    refs = list(refs)
    take = lambda n: [refs.pop(0) for _ in range(n)]
    halves = range(HALVES)
    xs = [take(HALVES) for _ in range(FILTER)]
    snds = [take(HALVES) for _ in range(FILTER)]
    ys = [take(HALVES) for _ in range(FILTER - 1)]
    s0 = take(HALVES)
    gp, gs, rb, bsem, xsem, csem, ssem, rsem, wss, wrs, pss, prs, ass, ars = refs
    me = lax.axis_index("row")
    mc = lax.axis_index("col")
    everyone = rows * parts
    linear = me * parts + mc
    hw = out.shape[2]
    width = hw * HALVES
    hops = hops_of(parts)
    rps = slice_of(width, rows)
    reducers = width // rps
    shifts = shifts_of(rows)
    groups = len(shifts)
    pn, pp = 0, lb * sc
    pperm = 2 * lb * sc
    pinv = pperm + lb
    pexn = pinv + lb
    pexp = pexn + groups * HALO
    bs = blk.shape[-1]
    chunks = lb // UNROLL

    def load(c):
        part = pl.ds(c * UNROLL, UNROLL)
        return pltpu.make_async_copy(blk.at[:, part], bm.at[:, part], bsem.at[c])

    def first(i, h):
        cut = sub.at[pl.ds(h * hw, hw), pl.ds(pl.multiple_of(i * bs, bs), bs)]
        return (pltpu.make_async_copy(cut, xs[0][h].at[i], xsem.at[h, i]),
                pltpu.make_async_copy(cut, s0[h].at[i], csem.at[h, i]))

    for h in halves:
        @pl.loop(0, lb)
        def _(i):
            a, b = first(i, h)
            b.start()
            a.start()

    @pl.loop(0, chunks)
    def _(c):
        load(c).start()

    barrier = pltpu.get_barrier_semaphore()

    @pl.loop(1, everyone)
    def _(e):
        to = lax.rem(linear + e, everyone)
        pl.semaphore_signal(barrier, inc=1, device_id=(to // parts, lax.rem(to, parts)),
                            device_id_type=pl.DeviceIdType.MESH)

    def copy(k, h, g):
        return pltpu.make_async_remote_copy(
            src_ref=snds[k][h].at[pl.ds(g * HALO, HALO)],
            dst_ref=xs[k][h].at[pl.ds(lb + g * HALO, HALO)],
            send_sem=ssem.at[k, h, g], recv_sem=rsem.at[k, h, g],
            device_id=(lax.rem(me - shifts[g] + rows, rows), mc),
            device_id_type=pl.DeviceIdType.MESH)

    def pack(k, h, g, source, base):
        for m in range(HALO):
            snds[k][h][g * HALO + m] = source[tab[base + g * HALO + m]].astype(bf16)

    for h in halves:
        @pl.loop(0, lb)
        def _(i):
            first(i, h)[1].wait()

        for g in range(groups):
            pack(0, h, g, s0[h], pexn)
        if h == 0:
            pl.semaphore_wait(barrier, everyone - 1)
        for g in range(groups):
            copy(0, h, g).start()

    for h in halves:
        @pl.loop(0, lb)
        def _(i):
            first(i, h)[0].wait()

    def product(k, h, j):
        i = j if k == FILTER - 1 else tab[pperm + j]
        own = tab[pinv + j] if k == FILTER - 1 else (i if k == 0 else j)
        base = pn if k == 0 else pp
        x = xs[k][h]
        left = jnp.concatenate([x[tab[base + i * sc + s]] for s in range(sc)], axis=1)
        right = jnp.concatenate([bm[s, i] for s in range(sc)], axis=0)
        acc = jnp.dot(left, right, preferred_element_type=f32)
        total = acc + ons[i] * x[own].astype(f32)
        if k == 0:
            return filter_scale * total
        prev = xs[0][h][i].astype(f32) if k == 1 else ys[k - 2][h][own]
        return 2.0 * filter_scale * total - prev

    def turn(piece, c):
        return lax.rem(c + (1 - piece // (parts // 2)) * (chunks // 2), chunks)

    def spread(n, h, c):
        bit, m = hops[n]
        piece = mc
        for b in (m & (1 << t) for t in range(m.bit_length())):
            if b:
                piece = flip(piece, b)
        part = out.at[piece * HALVES + h, pl.ds(turn(piece, c) * UNROLL, UNROLL)]
        return pltpu.make_async_remote_copy(
            src_ref=part, dst_ref=part, send_sem=wss.at[n, h, c], recv_sem=wrs.at[n, h, c],
            device_id=(me, flip(mc, bit)), device_id_type=pl.DeviceIdType.MESH)

    firsts = [n for n, (_, m) in enumerate(hops) if m == 0]

    @pl.loop(0, chunks)
    def _(c):
        load(c).wait()

    for k in range(FILTER):
        for h in halves:
            for g in range(groups):
                copy(k, h, g).wait_recv()

            @pl.loop(0, chunks)
            def _(c):
                if k < FILTER - 1:
                    for g in range(groups):
                        @pl.when(c == g + 1)
                        def _():
                            pack(k + 1, h, g, ys[k][h], pexp)
                for u in range(UNROLL):
                    j = (turn(mc, c) if k == FILTER - 1 else c) * UNROLL + u
                    value = product(k, h, j)
                    low = value.astype(bf16)
                    if k < FILTER - 1:
                        xs[k + 1][h][j] = low
                        ys[k][h][j] = value
                        if u == 1:
                            for g in range(groups):
                                @pl.when(c == g + 1)
                                def _():
                                    copy(k + 1, h, g).start()
                    else:
                        out[mc * HALVES + h, j] = low
                        if u == 1:
                            @pl.when(c > 0)
                            def _():
                                for n in firsts:
                                    spread(n, h, c - 1).start()
            if k == FILTER - 1:
                for n in firsts:
                    spread(n, h, chunks - 1).start()

    for k in range(FILTER):
        for h in halves:
            for g in range(groups):
                copy(k, h, g).wait_send()

    needs = {n: max(q for q in range(n) if sum(hops[q]) == m)
             for n, (_, m) in enumerate(hops) if m}
    def relay(lo, hi):
        for h in halves:
            @pl.loop(lo, hi)
            def _(c):
                got = set()
                for n in needs:
                    if needs[n] not in got:
                        spread(needs[n], h, c).wait_recv()
                        got.add(needs[n])
                    spread(n, h, c).start()

    def arrive(lo, hi, picked):
        for h in halves:
            @pl.loop(lo, hi)
            def _(c):
                for n in picked:
                    spread(n, h, c).wait_recv()

    top = parts // 2
    leaves = [n for n in range(len(hops)) if n not in needs.values()]
    near = [n for n in leaves if sum(hops[n]) < top]
    other = [n for n in leaves if sum(hops[n]) >= top]
    relay(0, chunks // 2)
    arrive(0, chunks, near)
    arrive(0, chunks // 2, other)

    gp[...] = jnp.zeros_like(gp)
    side = mc // top
    across = top * width

    def gram_part(where, start, count):
        cut = pl.ds(pl.multiple_of(where * across, across), across)

        @pl.loop(0, count)
        def _(c):
            first_row = start + c * 8
            left = jnp.concatenate([out[mc, first_row + u] for u in range(8)], axis=1)
            right = jnp.concatenate(
                [jnp.concatenate([out[where * top + q, first_row + u] for u in range(8)], axis=1)
                 for q in range(top)], axis=0)
            gp[:, cut] += lax.dot_general(left, right, (((1,), (1,)), ((), ())),
                                          preferred_element_type=f32)

    gram_part(side, 0, lb // 8)
    gram_part(1 - side, side * (lb // 2), lb // 16)

    def part_to(d):
        to = lax.rem(me + d, rows)
        lo = pl.multiple_of(to * rps, rps)
        return to, pltpu.make_async_remote_copy(
            src_ref=gp.at[pl.ds(lo, rps)], dst_ref=rb.at[d], send_sem=pss.at[d],
            recv_sem=prs.at[d], device_id=(to, mc), device_id_type=pl.DeviceIdType.MESH)

    def part_in(d):
        return pltpu.make_async_remote_copy(
            src_ref=gp.at[pl.ds(0, rps)], dst_ref=rb.at[d], send_sem=pss.at[d],
            recv_sem=prs.at[d], device_id=(lax.rem(me + 1, rows), mc),
            device_id_type=pl.DeviceIdType.MESH)

    def only(cond, run):
        if reducers == rows:
            run()
        else:
            pl.when(cond)(run)

    @pl.loop(1, rows)
    def _(d):
        to, c = part_to(d)
        only(to < reducers, lambda: c.start())

    def all_to(e, sender):
        to = lax.rem(linear + e, everyone)
        lo = pl.multiple_of((lax.rem(sender, parts) * reducers + sender // parts) * rps, rps)
        return pltpu.make_async_remote_copy(
            src_ref=gs, dst_ref=gram.at[pl.ds(lo, rps)], send_sem=ass.at[e],
            recv_sem=ars.at[e], device_id=(to // parts, lax.rem(to, parts)),
            device_id_type=pl.DeviceIdType.MESH)

    def reduce():
        lo = pl.multiple_of(me * rps, rps)
        total = gp[pl.ds(lo, rps)]
        for d in range(1, rows):
            part_in(d).wait_recv()
            total = total + rb[d]
        gs[...] = total
        gram[pl.ds(pl.multiple_of((mc * reducers + me) * rps, rps), rps)] = total

        @pl.loop(1, everyone)
        def _(e):
            all_to(e, linear).start()

    only(me < reducers, reduce)
    relay(chunks // 2, chunks)
    arrive(chunks // 2, chunks, other)
    for h in halves:
        @pl.loop(0, chunks)
        def _(c):
            for n in range(len(hops)):
                spread(n, h, c).wait_send()

    @pl.loop(1, rows)
    def _(d):
        to, c = part_to(d)
        only(to < reducers, lambda: c.wait_send())

    @pl.loop(1, everyone)
    def _(e):
        sender = lax.rem(linear - e + everyone, everyone)
        only(me < reducers, lambda: all_to(e, linear).wait_send())
        only(sender // parts < reducers, lambda: all_to(e, sender).wait_recv())


def filtered(subspace, onsite, blocks, cols):
    rows, parts = lax.axis_size("row"), lax.axis_size("col")
    me = lax.axis_index("row")
    everyone, hops = rows * parts, len(hops_of(parts))
    width = subspace.shape[0]
    sc, lb, bs, _ = blocks.shape
    groups = len(shifts_of(rows))
    tab = index_tables(cols, rows, me, lb)
    ext = lb + groups * HALO
    vm, dma = pltpu.VMEM, pltpu.SemaphoreType.DMA
    full, hw = parts * width, width // HALVES
    rps = slice_of(width, rows)
    return pl.pallas_call(
        functools.partial(filter_kernel, rows, parts, lb, sc),
        out_shape=(jax.ShapeDtypeStruct((parts * HALVES, lb, hw, bs), bf16),
                   jax.ShapeDtypeStruct((full, full), f32)),
        in_specs=[pl.BlockSpec(memory_space=pltpu.SMEM), pl.BlockSpec(memory_space=pl.ANY),
                  pl.BlockSpec(memory_space=pltpu.VMEM), pl.BlockSpec(memory_space=pl.ANY)],
        out_specs=[pl.BlockSpec(memory_space=pltpu.VMEM)] * 2,
        scratch_shapes=[vm((sc, lb, bs, bs), bf16)]
        + [vm((ext, hw, bs), bf16)] * (FILTER * HALVES)
        + [vm((groups * HALO, hw, bs), bf16)] * (FILTER * HALVES)
        + [vm((lb, hw, bs), f32)] * ((FILTER - 1) * HALVES)
        + [vm((lb, hw, bs), bf16)] * HALVES
        + [vm((width, full), f32), vm((rps, full), f32), vm((rows, rps, full), f32)]
        + [dma((lb // UNROLL,)), dma((HALVES, lb)), dma((HALVES, lb)),
           dma((FILTER, HALVES, groups)), dma((FILTER, HALVES, groups)),
           dma((hops, HALVES, lb // UNROLL)), dma((hops, HALVES, lb // UNROLL)),
           dma((rows,)), dma((rows,)), dma((everyone,)), dma((everyone,))],
        compiler_params=pltpu.CompilerParams(
            collective_id=0, has_side_effects=True, vmem_limit_bytes=56 * 1024 * 1024),
        name="filter",
    )(tab, subspace, onsite.reshape(lb, 1, bs), blocks)


def eliminate(src, up, low):
    n = src.shape[0]
    tiles = n // 8
    a = [src[8 * t:8 * t + 8, :] for t in range(tiles)]
    sub = lax.broadcasted_iota(jnp.int32, (8, n), 0)
    lane = lax.broadcasted_iota(jnp.int32, (8, n), 1)
    b = [jnp.where(lane == sub + 8 * t, 1.0, 0.0).astype(f32) for t in range(tiles)]

    def row(v, q):
        return jnp.broadcast_to(v[q:q + 1, :], (8, n))

    for p in range(tiles):
        cols = {t: [jnp.broadcast_to(a[t][:, 8 * p + q:8 * p + q + 1], (8, n)) for q in range(8)]
                for t in range(p, tiles)}
        pivots = jnp.ones((8, n), f32)
        for q in range(8):
            pivot = row(cols[p][q], q)
            pivots = jnp.where(sub == q, pivot, pivots)
            inverse = 1.0 / pivot
            right = [row(cols[p][k], q) for k in range(8)]
            arow, brow = row(a[p], q), row(b[p], q)
            for t in range(p, tiles):
                m = cols[t][q] * inverse
                if t == p:
                    m = jnp.where(sub > q, m, 0.0)
                for k in range(q + 1, 8):
                    cols[t][k] = cols[t][k] - m * right[k]
                a[t] = a[t] - m * arow
                b[t] = b[t] - m * brow
        scale = lax.rsqrt(pivots)
        up[8 * p:8 * p + 8, :] = jnp.where(lane >= sub + 8 * p, a[p] * scale, 0.0)
        low[8 * p:8 * p + 8, :] = b[p] * scale


def finish_kernel(root, col, stored, gram, basis, factor, work, up, low, inv, whole, sem):
    fetch = pltpu.make_async_copy(stored, whole, sem)
    fetch.start()
    parts, lb, _, bs = whole.shape
    width = basis.shape[0]
    full = gram.shape[0]
    half = full // 2
    exact = functools.partial(lax.dot_general, precision=lax.Precision.HIGHEST,
                              preferred_element_type=f32)
    nn, nt, tn = ((((1,), (0,)), ((), ())), (((1,), (1,)), ((), ())), (((0,), (0,)), ((), ())))
    corner = gram[:half, half:] + gram[half:, :half].T
    work[...] = gram[:half, :half]
    factor[half:, :half] = jnp.zeros((half, half), f32)
    inv[:half, half:] = jnp.zeros((half, half), f32)

    @pl.loop(0, 2)
    def _(i):
        eliminate(work, up.at[i], low.at[i])

        @pl.when(i == 0)
        def _():
            across = exact(low[0], corner, nn)
            factor[:half, half:] = across * (1.0 / root)
            work[...] = gram[half:, half:] - exact(across, across, tn)

    across = factor[:half, half:] * root
    inv[:half, :half] = low[0]
    inv[half:, half:] = low[1]
    inv[half:, :half] = -exact(low[1], exact(across, low[0], tn), nn)
    factor[:half, :half] = up[0] * (1.0 / root)
    factor[half:, half:] = up[1] * (1.0 / root)

    mine = inv[pl.ds(pl.multiple_of(col[0] * width, width), width), :] * root
    high = mine.astype(bf16)
    rest = mine - high.astype(f32)
    mid = rest.astype(bf16)
    last = (rest - mid.astype(f32)).astype(bf16)
    left = jnp.concatenate([high, mid, last], axis=0)

    fetch.wait()
    for k in range(lb):
        right = jnp.concatenate([whole[q, k] for q in range(parts)], axis=0)
        r = jnp.dot(left, right, preferred_element_type=f32)
        basis[:, k * bs:(k + 1) * bs] = r[:width] + (r[width:2 * width] + r[2 * width:])


def body(subspace, onsite, blocks, cols):
    row_count = lax.axis_size("row")
    part_width, local_rows = subspace.shape
    whole, gram = filtered(subspace, onsite, blocks, cols)
    full = gram.shape[0]
    half = full // 2
    root = math.sqrt(row_count * local_rows)
    vm = pltpu.VMEM
    return pl.pallas_call(
        functools.partial(finish_kernel, root),
        out_shape=(jax.ShapeDtypeStruct((part_width, local_rows), f32),
                   jax.ShapeDtypeStruct((full, full), f32)),
        in_specs=[pl.BlockSpec(memory_space=pltpu.SMEM), pl.BlockSpec(memory_space=pltpu.HBM),
                  pl.BlockSpec(memory_space=vm)],
        out_specs=[pl.BlockSpec(memory_space=vm)] * 2,
        scratch_shapes=[vm((half, half), f32), vm((2, half, half), f32), vm((2, half, half), f32),
                        vm((full, full), f32), vm(whole.shape, bf16), pltpu.SemaphoreType.DMA],
        compiler_params=pltpu.CompilerParams(vmem_limit_bytes=32 * 1024 * 1024),
        name="finish",
    )(lax.axis_index("col").astype(jnp.int32).reshape(1), whole, gram)


def solution(mesh):
    in_specs = (P("col", "row"), P("row"), P(None, "row", None, None), P())
    out_specs = (P("col", "row"), P())
    return jax.shard_map(body, mesh=mesh, in_specs=in_specs, out_specs=out_specs, check_vma=False)
```

profile of v0, /device:TPU:0, one launch (start us, length us, event | category | flops | bytes accessed | tf_op | source)
XLA Modules:
  0.0 83.1 jit_solution(16090311377207032723)
XLA Ops:
  0.7 0.1 add_multiply_fusion
  0.8 0.9 %constant_dynamic-slice_fusion.4 = (s32[32,20]{0,1:T(8,128)S(1)}, s32[32,20]{0,1:T(8,128)S(1)}, s32[32,20]{0,1:T(8,128)S(1)}, s32[32,20]{0,1:T(8,128)S(1)}, s32[32,20]{0,1:T(8,128)S(1)}) fusion(s32[256,20]{0,1:T(8,128)} %param.7, s32[]{:T(128)S(6)} %select_n.45, s32[]{:T(128)S(6)} %select_n.47, s32[]{:T(128)S(6)} %select_n.46, s32[]{:T(128)S(6)} %select_n.49, ...), kind=kLoop, calls=%fused_computation.28 | loop fusion | bytes 25620 | tf_op jit(solution)/shard_map/dynamic_slice | solution.py:28
  1.7 0.1 copy.11
  1.8 0.1 reshape.115
  1.9 0.1 copy.13
  1.9 0.1 stack_reshape.13
  2.1 0.1 copy.12
  2.1 0.1 stack_reshape.12
  2.3 0.1 copy.15
  2.3 0.1 stack_reshape.15
  2.4 0.1 copy.14
  2.5 0.1 stack_reshape.14
  2.6 0.1 add_subtract_fusion
  2.7 0.2 fusion
  3.0 0.1 convert_reduce_fusion
  3.1 0.1 fusion.4
  3.2 0.1 select_reduce_fusion
  3.3 0.1 convert_reduce_fusion.1
  3.4 0.1 select_reduce_fusion.2
  3.5 0.2 select_reduce_fusion.3
  3.7 0.1 reshape.117
  3.8 0.1 reshape.116
  3.9 0.1 select_reduce_fusion.1
  4.0 0.7 concatenate.11.tab
  4.7 64.7 %filter.1 = (bf16[4,32,64,128]{3,2,1,0:T(8,128)(2,1)}, f32[256,256]{1,0:T(8,128)}) custom-call(s32[1376]{0:T(1024)} %concatenate.11.tab, bf16[64,4096]{1,0:T(8,128)(2,1)} %sub.54, f32[32,1,128]{2,1,0:T(1,128)} %bitcast.6, bf16[20,32,128,128]{3,2,1,0:T(8,128)(2,1)} %blk.1), custom_call_target="tpu_custom_call" | custom-call | tf_op jit(solution)/shard_map/filter/pallas_call | solution.py:366
  69.4 0.0 copy-start
  69.4 1.6 %copy-done = bf16[4,32,64,128]{3,2,1,0:T(8,128)(2,1)S(1)} copy-done((bf16[4,32,64,128]{3,2,1,0:T(8,128)(2,1)S(1)}, bf16[4,32,64,128]{3,2,1,0:T(8,128)(2,1)}, u32[]{:S(2)}) %copy-start) | copy-done | bytes 2097176
  71.0 0.0 copy-start.1
  71.0 0.9 %copy-done.1 = f32[256,256]{1,0:T(8,128)S(1)} copy-done((f32[256,256]{1,0:T(8,128)S(1)}, f32[256,256]{1,0:T(8,128)}, u32[]{:S(2)}) %copy-start.1) | copy-done | bytes 262168
  71.9 11.2 %finish.1 = (f32[64,4096]{1,0:T(8,128)}, f32[256,256]{1,0:T(8,128)}) custom-call(s32[1]{0:T(128)} %bitcast.col, bf16[4,32,64,128]{3,2,1,0:T(8,128)(2,1)S(1)} %copy-done, f32[256,256]{1,0:T(8,128)S(1)} %copy-done.1), custom_call_target="tpu_custom_call" | custom-call | tf_op jit(solution)/shard_map/finish/pallas_call | solution.py:477
  (7 shorter events, 0.1 us)
Async XLA Ops:
  69.4 1.6 %copy-start = (bf16[4,32,64,128]{3,2,1,0:T(8,128)(2,1)S(1)}, bf16[4,32,64,128]{3,2,1,0:T(8,128)(2,1)}, u32[]{:S(2)}) copy-start(bf16[4,32,64,128]{3,2,1,0:T(8,128)(2,1)} %get-tuple-element.4.stored) | copy-start | bytes 6291460
  71.0 0.9 %copy-start.1 = (f32[256,256]{1,0:T(8,128)S(1)}, f32[256,256]{1,0:T(8,128)}, u32[]{:S(2)}) copy-start(f32[256,256]{1,0:T(8,128)} %get-tuple-element.5.gram) | copy-start | bytes 786436
where the time goes:
time: 83.4 us; the launch traced here: 83.1 us
  Pallas kernels  75.9 us (91%)
  local copies, waits for them, and re-layouts  5.24 us (6%)
  other arithmetic  1.26 us (2%)
    pallas_call x1, Pallas kernels, filtered(): pl.pallas_call(functools.partial(filter_kernel, rows, parts, lb, sc), out...  64.7 us
    pallas_call x1, Pallas kernels, body(): pl.pallas_call(functools.partial(finish_kernel, root), out_shape=(jax.Sha...  11.2 us
    unnamed x4, local copies, waits for them, and re-layouts  2.53 us

commit v1 on v0

--- a/solution.py
+++ b/solution.py
@@ -163,18 +163,34 @@
         def _(i):
             first(i, h)[0].wait()
 
-    def product(k, h, j):
+    def place(k, j):
         i = j if k == FILTER - 1 else tab[pperm + j]
         own = tab[pinv + j] if k == FILTER - 1 else (i if k == 0 else j)
+        return i, own
+
+    def feed(k, first_row, accs):
         base = pn if k == 0 else pp
-        x = xs[k][h]
-        left = jnp.concatenate([x[tab[base + i * sc + s]] for s in range(sc)], axis=1)
-        right = jnp.concatenate([bm[s, i] for s in range(sc)], axis=0)
-        acc = jnp.dot(left, right, preferred_element_type=f32)
-        total = acc + ons[i] * x[own].astype(f32)
+        x = xs[k][0]
+        at = [place(k, first_row + u)[0] for u in range(UNROLL)]
+        for t in range(sc // 2):
+            for m in range(2):
+                pair = at[2 * m:2 * m + 2]
+                pltpu.matmul_push_rhs(jnp.concatenate(
+                    [jnp.concatenate([bm[2 * t, i], bm[2 * t + 1, i]], axis=0) for i in pair],
+                    axis=1), t % 2, m)
+                for u, i in enumerate(pair):
+                    left = jnp.concatenate(
+                        [x[tab[base + i * sc + 2 * t + s]] for s in range(2)], axis=1)
+                    pltpu.matmul_acc_lhs(accs[m][u], left,
+                                         load_staged_rhs=t % 2 if u == 0 else None)
+
+    def settle(k, row, acc, u):
+        i, own = place(k, row)
+        total = pltpu.matmul_pop(acc)[:, u * bs:(u + 1) * bs]
+        total = total + ons[i] * xs[k][0][own].astype(f32)
         if k == 0:
             return filter_scale * total
-        prev = xs[0][h][i].astype(f32) if k == 1 else ys[k - 2][h][own]
+        prev = xs[0][0][i].astype(f32) if k == 1 else ys[k - 2][0][own]
         return 2.0 * filter_scale * total - prev
 
     def turn(piece, c):
@@ -197,40 +213,63 @@
     def _(c):
         load(c).wait()
 
-    for k in range(FILTER):
-        for h in halves:
+    def keep(k, j, value):
+        low = value.astype(bf16)
+        if k < FILTER - 1:
+            xs[k + 1][0][j] = low
+            ys[k][0][j] = value
+        else:
+            out[mc, j] = low
+
+    def rows_of(k, c):
+        return (turn(mc, c) if k == FILTER - 1 else c) * UNROLL
+
+    def chunk(k, c, accs):
+        for m in range(2):
+            for u in range(2):
+                j = rows_of(k, c) + 2 * m + u
+                keep(k, j, settle(k, j, accs[m][u], u))
+
+    def filtering(*flat):
+        sets = [[flat[4 * q + 2 * m:4 * q + 2 * m + 2] for m in range(2)] for q in range(2)]
+        for k in range(FILTER):
             for g in range(groups):
-                copy(k, h, g).wait_recv()
-
-            @pl.loop(0, chunks)
-            def _(c):
-                if k < FILTER - 1:
-                    for g in range(groups):
-                        @pl.when(c == g + 1)
-                        def _():
-                            pack(k + 1, h, g, ys[k][h], pexp)
-                for u in range(UNROLL):
-                    j = (turn(mc, c) if k == FILTER - 1 else c) * UNROLL + u
-                    value = product(k, h, j)
-                    low = value.astype(bf16)
-                    if k < FILTER - 1:
-                        xs[k + 1][h][j] = low
-                        ys[k][h][j] = value
-                        if u == 1:
-                            for g in range(groups):
-                                @pl.when(c == g + 1)
-                                def _():
-                                    copy(k + 1, h, g).start()
-                    else:
-                        out[mc * HALVES + h, j] = low
-                        if u == 1:
-                            @pl.when(c > 0)
-                            def _():
-                                for n in firsts:
-                                    spread(n, h, c - 1).start()
+                copy(k, 0, g).wait_recv()
+            ahead = groups if k < FILTER - 1 else 0
+            for c in range(0, ahead, 2):
+                for q in range(2):
+                    feed(k, rows_of(k, c + q), sets[q])
+                if c:
+                    copy(k + 1, 0, c - 1).start()
+                for q in range(2):
+                    chunk(k, c + q, sets[q])
+                    if q:
+                        copy(k + 1, 0, c).start()
+                    pack(k + 1, 0, c + q, ys[k][0], pexp)
+
+            @pl.loop(ahead // 2, chunks // 2)
+            def _(cc):
+                for q in range(2):
+                    feed(k, rows_of(k, 2 * cc + q), sets[q])
+                if ahead:
+                    @pl.when(cc == ahead // 2)
+                    def _():
+                        copy(k + 1, 0, ahead - 1).start()
+                for q in range(2):
+                    chunk(k, 2 * cc + q, sets[q])
+                if k == FILTER - 1:
+                    @pl.when(cc > 0)
+                    def _():
+                        for n in firsts:
+                            for q in range(2):
+                                spread(n, 0, 2 * cc - 2 + q).start()
             if k == FILTER - 1:
                 for n in firsts:
-                    spread(n, h, chunks - 1).start()
+                    for q in range(2):
+                        spread(n, 0, chunks - 2 + q).start()
+
+    pl.run_scoped(filtering, *[pltpu.ACC(m)((width, 2 * bs), f32)
+                               for _ in range(2) for m in range(2) for _ in range(2)])
 
     for k in range(FILTER):
         for h in halves:
@@ -265,25 +304,44 @@
     arrive(0, chunks, near)
     arrive(0, chunks // 2, other)
 
-    gp[...] = jnp.zeros_like(gp)
     side = mc // top
-    across = top * width
-
-    def gram_part(where, start, count):
-        cut = pl.ds(pl.multiple_of(where * across, across), across)
-
-        @pl.loop(0, count)
+    half = lb // 2
+
+    def tall(q, first_row):
+        return jnp.concatenate([out[q, first_row], out[q, first_row + 1]], axis=1)
+
+    def gramming(*accs):
+        both, one, two = [accs[2 * n:2 * n + 2] for n in range(3)]
+
+        @pl.loop(0, half // 4)
         def _(c):
-            first_row = start + c * 8
-            left = jnp.concatenate([out[mc, first_row + u] for u in range(8)], axis=1)
-            right = jnp.concatenate(
-                [jnp.concatenate([out[where * top + q, first_row + u] for u in range(8)], axis=1)
-                 for q in range(top)], axis=0)
-            gp[:, cut] += lax.dot_general(left, right, (((1,), (1,)), ((), ())),
-                                          preferred_element_type=f32)
-
-    gram_part(side, 0, lb // 8)
-    gram_part(1 - side, side * (lb // 2), lb // 16)
+            for m in range(2):
+                row = side * half + c * 4 + 2 * m
+                pltpu.matmul_push_rhs(
+                    jnp.concatenate([tall(q, row) for q in range(parts)], axis=0),
+                    0, m, transpose=True)
+                pltpu.matmul_acc_lhs(both[m], tall(mc, row), load_staged_rhs=0)
+
+        @pl.loop(0, half // 8)
+        def _(c):
+            for m in range(2):
+                row = (1 - side) * half + c * 8 + 4 * m
+                pltpu.matmul_push_rhs(
+                    jnp.concatenate([tall(side * top + q, row + r)
+                                     for r in (0, 2) for q in range(top)], axis=0),
+                    0, m, transpose=True)
+                pltpu.matmul_acc_lhs(one[m], tall(mc, row), load_staged_rhs=0)
+                pltpu.matmul_acc_lhs(two[m], tall(mc, row + 2))
+
+        across = top * width
+        gp[...] = pltpu.matmul_pop(both[0]) + pltpu.matmul_pop(both[1])
+        cut = pl.ds(pl.multiple_of(side * across, across), across)
+        near_sum = [pltpu.matmul_pop(one[m])[:, :across] + pltpu.matmul_pop(two[m])[:, across:]
+                    for m in range(2)]
+        gp[:, cut] += near_sum[0] + near_sum[1]
+
+    pl.run_scoped(gramming, *[pltpu.ACC(m)((width, parts * width), f32)
+                              for _ in range(3) for m in range(2)])
 
     def part_to(d):
         to = lax.rem(me + d, rows)
@@ -483,7 +541,7 @@
         out_specs=[pl.BlockSpec(memory_space=vm)] * 2,
         scratch_shapes=[vm((half, half), f32), vm((2, half, half), f32), vm((2, half, half), f32),
                         vm((full, full), f32), vm(whole.shape, bf16), pltpu.SemaphoreType.DMA],
-        compiler_params=pltpu.CompilerParams(vmem_limit_bytes=32 * 1024 * 1024),
+        compiler_params=pltpu.CompilerParams(vmem_limit_bytes=60 * 1024 * 1024),
         name="finish",
     )(lax.axis_index("col").astype(jnp.int32).reshape(1), whole, gram)
 

time: 83.4 us -> 80.7 us (0.968)
  local copies, waits for them, and re-layouts: 5.24 us -> 2.7 us
    unnamed x4 -> x0, local copies, waits for them, and re-layouts: 2.53 us -> none
    pallas_call x1, Pallas kernels: 64.7 us -> 63.4 us  [filtered(): pl.pallas_call(functools.partial(filter_kernel, rows, parts, lb, sc), out...]
    pallas_call x1, Pallas kernels: 11.2 us -> 12.2 us  [body(): pl.pallas_call(functools.partial(finish_kernel, root), out_shape=(jax.Sha...]
where the time goes in v1:
time: 80.7 us; the launch traced here: 80.4 us
  Pallas kernels  75.6 us (94%)
  local copies, waits for them, and re-layouts  2.7 us (3%)
  other arithmetic  1.26 us (2%)
  between operations  0.9 us (1%)
    pallas_call x1, Pallas kernels, filtered(): pl.pallas_call(functools.partial(filter_kernel, rows, parts, lb, sc), out...  63.4 us
    pallas_call x1, Pallas kernels, body(): pl.pallas_call(functools.partial(finish_kernel, root), out_shape=(jax.Sha...  12.2 us

profile of v1, /device:TPU:0, one launch (start us, length us, event | category | flops | bytes accessed | tf_op | source)
XLA Modules:
  0.0 80.4 jit_solution(5198554775882668164)
XLA Ops:
  0.7 0.1 add_multiply_fusion
  0.8 0.9 %constant_dynamic-slice_fusion.4 = (s32[32,20]{0,1:T(8,128)S(1)}, s32[32,20]{0,1:T(8,128)S(1)}, s32[32,20]{0,1:T(8,128)S(1)}, s32[32,20]{0,1:T(8,128)S(1)}, s32[32,20]{0,1:T(8,128)S(1)}) fusion(s32[256,20]{0,1:T(8,128)} %param.7, s32[]{:T(128)S(6)} %select_n.45, s32[]{:T(128)S(6)} %select_n.47, s32[]{:T(128)S(6)} %select_n.46, s32[]{:T(128)S(6)} %select_n.49, ...), kind=kLoop, calls=%fused_computation.28 | loop fusion | bytes 25620 | tf_op jit(solution)/shard_map/dynamic_slice | solution.py:28
  1.7 0.1 copy.11
  1.8 0.1 reshape.115
  1.9 0.1 copy.13
  1.9 0.1 stack_reshape.13
  2.1 0.1 copy.12
  2.1 0.1 stack_reshape.12
  2.3 0.1 copy.15
  2.3 0.1 stack_reshape.15
  2.4 0.1 copy.14
  2.5 0.1 stack_reshape.14
  2.6 0.1 add_subtract_fusion
  2.7 0.2 fusion
  3.0 0.1 convert_reduce_fusion
  3.1 0.1 fusion.4
  3.2 0.1 select_reduce_fusion
  3.3 0.1 convert_reduce_fusion.1
  3.4 0.1 select_reduce_fusion.2
  3.5 0.2 select_reduce_fusion.3
  3.7 0.1 reshape.117
  3.8 0.1 reshape.116
  3.9 0.1 select_reduce_fusion.1
  4.0 0.7 concatenate.11.tab
  4.7 63.4 %filter.1 = (bf16[4,32,64,128]{3,2,1,0:T(8,128)(2,1)}, f32[256,256]{1,0:T(8,128)}) custom-call(s32[1376]{0:T(1024)} %concatenate.11.tab, bf16[64,4096]{1,0:T(8,128)(2,1)} %sub.54, f32[32,1,128]{2,1,0:T(1,128)} %bitcast.6, bf16[20,32,128,128]{3,2,1,0:T(8,128)(2,1)} %blk.1), custom_call_target="tpu_custom_call" | custom-call | tf_op jit(solution)/shard_map/filter/pallas_call | solution.py:424
  68.1 12.2 %finish.1 = (f32[64,4096]{1,0:T(8,128)}, f32[256,256]{1,0:T(8,128)}) custom-call(s32[1]{0:T(128)} %bitcast.col, bf16[4,32,64,128]{3,2,1,0:T(8,128)(2,1)} %get-tuple-element.4.stored, f32[256,256]{1,0:T(8,128)} %get-tuple-element.5.gram), custom_call_target="tpu_custom_call" | custom-call | tf_op jit(solution)/shard_map/finish/pallas_call | solution.py:535
  (7 shorter events, 0.1 us)

commit v2 on v1

--- a/solution.py
+++ b/solution.py
@@ -21,44 +21,88 @@
     return (rows // 2, 2, 1, -1)
 
 
-def index_tables(cols, rows, me, lb):
-    sc = cols.shape[1]
+def bits_below(k):
+    return lax.shift_left(jnp.ones_like(k), k) - 1
+
+
+def ones_in(x):
+    return lax.population_count(x)
+
+
+def folded(x, axis):
+    step = x.shape[axis] // 2
+    while step:
+        x = x | pltpu.roll(x, step, axis)
+        step //= 2
+    return x
+
+
+def tiles_of(sc):
+    return list(range(0, sc - 7, 8)) + ([sc - 8] if sc % 8 else [])
+
+
+def masks_of(cvm, rows, me, lb, sc):
     shifts = shifts_of(rows)
     groups = len(shifts)
-    own = lax.dynamic_slice_in_dim(cols, me * lb, lb, 0).reshape(-1)
-    askers = [
-        lax.dynamic_slice_in_dim(cols, lax.rem(me - d + rows, rows) * lb, lb, 0).reshape(-1)
-        for d in shifts
-    ]
-    owners = jnp.stack([lax.rem(me + d + rows, rows) for d in shifts])
-    k = jnp.arange(lb, dtype=jnp.int32)
-    wanted = own[None, :] - owners[:, None] * lb
-    asked = jnp.stack(askers) - me * lb
-    rel = jnp.concatenate([wanted, asked], 0)
-    hit = jnp.any(rel[:, :, None] == k, axis=1)
-    before = (k[:, None] < k[None, :])
-    rank = jnp.sum((hit[:, :, None] & before[None]).astype(jnp.int32), axis=1)
-    hit_e, rank_e = hit[groups:], rank[groups:]
-    g = jnp.arange(groups, dtype=jnp.int32)
-    key = jnp.min(jnp.where(hit_e, g[:, None], groups), axis=0)
-    ahead = (key[:, None] < key[None, :]) | ((key[:, None] == key[None, :]) & before)
-    inv = jnp.sum(ahead.astype(jnp.int32), axis=0)
-    perm = jnp.sum(jnp.where(inv[None, :] == k[:, None], k[None, :], 0), axis=1)
-    m = jnp.arange(HALO, dtype=jnp.int32)
-    pick = hit_e[:, None, :] & (rank_e[:, None, :] == m[:, None])
-    exp_n = jnp.sum(jnp.where(pick, k, 0), axis=-1)
-    exp_p = jnp.sum(jnp.where(pick, inv, 0), axis=-1)
-    slot = lb + HALO * g[:, None] + rank[:groups]
-    match = wanted[:, :, None] == k
-    far = jnp.sum(jnp.where(match, slot[:, None, :], 0), axis=(0, 2))
-    near = own - me * lb
-    mine = (near >= 0) & (near < lb)
-    near_p = jnp.sum(jnp.where(near[:, None] == k, inv, 0), axis=1)
-    pos_n = jnp.where(mine, near, far)
-    pos_p = jnp.where(mine, near_p, far)
-    return jnp.concatenate(
-        [pos_n, pos_p, perm, inv, exp_n.reshape(-1), exp_p.reshape(-1)]
-    ).astype(jnp.int32)
+    lane = lax.broadcasted_iota(jnp.int32, (8, 128), 1)
+    sub = lax.broadcasted_iota(jnp.int32, (8, 128), 0)
+    per = 128 // lb
+
+    def picked(device, owners):
+        start = pl.multiple_of(device // per * 128, 128)
+        live = lane // lb == lax.rem(device, per)
+        found = [jnp.zeros((8, 128), jnp.int32) for _ in owners]
+        for o in tiles_of(sc):
+            v = cvm[o:o + 8, pl.ds(start, 128)]
+            for n, owner in enumerate(owners):
+                rel = v - owner * lb
+                hit = live & (rel >= 0) & (rel < lb)
+                found[n] = found[n] | jnp.where(
+                    hit, lax.shift_left(jnp.ones_like(rel), rel & (lb - 1)), 0)
+        return found
+
+    found = picked(me, [lax.rem(me + d + rows, rows) for d in shifts])
+    for d in shifts:
+        found += picked(lax.rem(me - d + rows, rows), [me])
+    both = jnp.zeros((8, 128), jnp.int32)
+    for n, x in enumerate(found):
+        both = jnp.where(sub == n, folded(x, 0), both)
+    assert groups == 4
+    return folded(both, 1)
+
+
+def mask_row(masks, n):
+    return jnp.broadcast_to(masks[n:n + 1, :], (8, 128))
+
+
+def byte_of(word, n, limit):
+    return lax.shift_right_logical(word, 8 * n) & (limit - 1)
+
+
+def packed_exports(masks, lb, names):
+    k = lax.broadcasted_iota(jnp.int32, (8, 128), 1)
+    low = jnp.minimum(k, lb - 1)
+    hit = (k < lb) & ((lax.shift_right_logical(masks, low) & 1) == 1)
+    rank = ones_in(masks & bits_below(low))
+    word = jnp.zeros((8, 128), jnp.int32)
+    for m in range(HALO):
+        word = word | jnp.where(hit & (rank == m), lax.shift_left(names, jnp.full_like(names, 8 * m)), 0)
+    return folded(word, 1)
+
+
+def order_of(masks, groups, at):
+    taken = jnp.zeros((8, 128), jnp.int32)
+    base = jnp.zeros((8, 128), jnp.int32)
+    place = jnp.zeros((8, 128), jnp.int32)
+    below = bits_below(at)
+    for g in range(groups + 1):
+        left = ~taken
+        mine = left if g == groups else mask_row(masks, groups + g) & left
+        here = (lax.shift_right_logical(mine, at) & 1) == 1
+        place = jnp.where(here, base + ones_in(mine & below), place)
+        base = base + ones_in(mine)
+        taken = taken | mine
+    return place
 
 
 def flip(c, bit):
@@ -78,7 +122,7 @@
     return max(8, width // rows)
 
 
-def filter_kernel(rows, parts, lb, sc, tab, sub, ons, blk, out, gram, bm, *refs):
+def filter_kernel(rows, parts, lb, sc, cols, sub, ons_in, blk, stored, gram, bm, *refs):
     refs = list(refs)
     take = lambda n: [refs.pop(0) for _ in range(n)]
     halves = range(HALVES)
@@ -86,23 +130,19 @@
     snds = [take(HALVES) for _ in range(FILTER)]
     ys = [take(HALVES) for _ in range(FILTER - 1)]
     s0 = take(HALVES)
-    gp, gs, rb, bsem, xsem, csem, ssem, rsem, wss, wrs, pss, prs, ass, ars = refs
+    (out, ons, cvm, early_v, late_v, early, late, gp, gs, rb, bsem, xsem, csem, ssem, rsem,
+     wss, wrs, pss, prs, ass, ars, tsem, osem) = refs
     me = lax.axis_index("row")
     mc = lax.axis_index("col")
     everyone = rows * parts
     linear = me * parts + mc
-    hw = out.shape[2]
-    width = hw * HALVES
+    width = sub.shape[0]
+    hw = width // HALVES
     hops = hops_of(parts)
     rps = slice_of(width, rows)
     reducers = width // rps
     shifts = shifts_of(rows)
     groups = len(shifts)
-    pn, pp = 0, lb * sc
-    pperm = 2 * lb * sc
-    pinv = pperm + lb
-    pexn = pinv + lb
-    pexp = pexn + groups * HALO
     bs = blk.shape[-1]
     chunks = lb // UNROLL
 
@@ -115,6 +155,16 @@
         return (pltpu.make_async_copy(cut, xs[0][h].at[i], xsem.at[h, i]),
                 pltpu.make_async_copy(cut, s0[h].at[i], csem.at[h, i]))
 
+    barrier = pltpu.get_barrier_semaphore()
+
+    @pl.loop(1, everyone)
+    def _(e):
+        to = lax.rem(linear + e, everyone)
+        pl.semaphore_signal(barrier, inc=1, device_id=(to // parts, lax.rem(to, parts)),
+                            device_id_type=pl.DeviceIdType.MESH)
+
+    named = pltpu.make_async_copy(cols, cvm, tsem.at[0])
+    named.start()
     for h in halves:
         @pl.loop(0, lb)
         def _(i):
@@ -122,17 +172,53 @@
             b.start()
             a.start()
 
+    energies = pltpu.make_async_copy(ons_in, ons, tsem.at[1])
+    energies.start()
+
     @pl.loop(0, chunks)
     def _(c):
         load(c).start()
 
-    barrier = pltpu.get_barrier_semaphore()
-
-    @pl.loop(1, everyone)
-    def _(e):
-        to = lax.rem(linear + e, everyone)
-        pl.semaphore_signal(barrier, inc=1, device_id=(to // parts, lax.rem(to, parts)),
-                            device_id_type=pl.DeviceIdType.MESH)
+    named.wait()
+    masks = masks_of(cvm, rows, me, lb, sc)
+    lane = lax.broadcasted_iota(jnp.int32, (8, 128), 1)
+    sublane = lax.broadcasted_iota(jnp.int32, (8, 128), 0)
+    early_v[...] = packed_exports(masks, lb, lane)
+    to_early = pltpu.make_async_copy(early_v, early, tsem.at[2])
+    to_early.start()
+
+    inverse = order_of(masks, groups, jnp.minimum(lane, lb - 1))
+    late_v[0:8, :] = packed_exports(masks, lb, inverse)
+    word = jnp.zeros((8, 128), jnp.int32)
+    for q in range(lb // 8):
+        word = word | jnp.where((lane < lb) & (inverse == 8 * q + sublane),
+                                lax.shift_left(lane, jnp.full_like(lane, 8 * q)), 0)
+    late_v[8:16, :] = folded(word, 1)
+    late_v[16:24, :] = inverse
+    per = 128 // lb
+    start = pl.multiple_of(me // per * 128, 128)
+    for o in tiles_of(sc):
+        v = cvm[o:o + 8, pl.ds(start, 128)]
+        rel = v - me * lb
+        near = (rel >= 0) & (rel < lb)
+        low = rel & (lb - 1)
+        far = jnp.zeros((8, 128), jnp.int32)
+        for g, d in enumerate(shifts):
+            there = v - lax.rem(me + d + rows, rows) * lb
+            at = there & (lb - 1)
+            far = jnp.where((there >= 0) & (there < lb),
+                            lb + HALO * g + ones_in(mask_row(masks, g) & bits_below(at)), far)
+        late_v[24 + o:32 + o, :] = jnp.where(near, low, far)
+        late_v[24 + sc + o:32 + sc + o, :] = jnp.where(near, order_of(masks, groups, low), far)
+    to_late = pltpu.make_async_copy(late_v, late, tsem.at[3])
+    shift = lax.rem(me, per) * lb
+    pn, pp, span = 24, 24 + sc, xs[0][0].shape[0]
+
+    def export(k, g, m):
+        return byte_of(early[groups + g, 0] if k == 0 else late[groups + g, 0], m, lb)
+
+    def permuted(j):
+        return byte_of(late[8 + lax.rem(j, 8), 0], j // 8, lb)
 
     def copy(k, h, g):
         return pltpu.make_async_remote_copy(
@@ -142,30 +228,35 @@
             device_id=(lax.rem(me - shifts[g] + rows, rows), mc),
             device_id_type=pl.DeviceIdType.MESH)
 
-    def pack(k, h, g, source, base):
+    def pack(k, h, g, source):
         for m in range(HALO):
-            snds[k][h][g * HALO + m] = source[tab[base + g * HALO + m]].astype(bf16)
+            snds[k][h][g * HALO + m] = source[export(k, g, m)].astype(bf16)
 
     for h in halves:
         @pl.loop(0, lb)
         def _(i):
             first(i, h)[1].wait()
 
+        to_early.wait()
         for g in range(groups):
-            pack(0, h, g, s0[h], pexn)
+            pack(0, h, g, s0[h])
         if h == 0:
             pl.semaphore_wait(barrier, everyone - 1)
         for g in range(groups):
             copy(0, h, g).start()
 
+    to_late.start()
     for h in halves:
         @pl.loop(0, lb)
         def _(i):
             first(i, h)[0].wait()
 
+    energies.wait()
+    to_late.wait()
+
     def place(k, j):
-        i = j if k == FILTER - 1 else tab[pperm + j]
-        own = tab[pinv + j] if k == FILTER - 1 else (i if k == 0 else j)
+        i = j if k == FILTER - 1 else permuted(j)
+        own = late[16, j] & (lb - 1) if k == FILTER - 1 else (i if k == 0 else j)
         return i, own
 
     def feed(k, first_row, accs):
@@ -180,7 +271,7 @@
                     axis=1), t % 2, m)
                 for u, i in enumerate(pair):
                     left = jnp.concatenate(
-                        [x[tab[base + i * sc + 2 * t + s]] for s in range(2)], axis=1)
+                        [x[late[base + 2 * t + s, shift + i] & (span - 1)] for s in range(2)], axis=1)
                     pltpu.matmul_acc_lhs(accs[m][u], left,
                                          load_staged_rhs=t % 2 if u == 0 else None)
 
@@ -245,7 +336,7 @@
                     chunk(k, c + q, sets[q])
                     if q:
                         copy(k + 1, 0, c).start()
-                    pack(k + 1, 0, c + q, ys[k][0], pexp)
+                    pack(k + 1, 0, c + q, ys[k][0])
 
             @pl.loop(ahead // 2, chunks // 2)
             def _(cc):
@@ -391,6 +482,8 @@
     only(me < reducers, reduce)
     relay(chunks // 2, chunks)
     arrive(chunks // 2, chunks, other)
+    keep_all = pltpu.make_async_copy(out, stored, osem)
+    keep_all.start()
     for h in halves:
         @pl.loop(0, chunks)
         def _(c):
@@ -407,17 +500,17 @@
         sender = lax.rem(linear - e + everyone, everyone)
         only(me < reducers, lambda: all_to(e, linear).wait_send())
         only(sender // parts < reducers, lambda: all_to(e, sender).wait_recv())
+    keep_all.wait()
 
 
 def filtered(subspace, onsite, blocks, cols):
     rows, parts = lax.axis_size("row"), lax.axis_size("col")
-    me = lax.axis_index("row")
     everyone, hops = rows * parts, len(hops_of(parts))
     width = subspace.shape[0]
     sc, lb, bs, _ = blocks.shape
     groups = len(shifts_of(rows))
-    tab = index_tables(cols, rows, me, lb)
-    ext = lb + groups * HALO
+    assert lb in (8, 16, 32) and sc >= 8
+    ext = pl.next_power_of_2(lb + groups * HALO)
     vm, dma = pltpu.VMEM, pltpu.SemaphoreType.DMA
     full, hw = parts * width, width // HALVES
     rps = slice_of(width, rows)
@@ -425,23 +518,25 @@
         functools.partial(filter_kernel, rows, parts, lb, sc),
         out_shape=(jax.ShapeDtypeStruct((parts * HALVES, lb, hw, bs), bf16),
                    jax.ShapeDtypeStruct((full, full), f32)),
-        in_specs=[pl.BlockSpec(memory_space=pltpu.SMEM), pl.BlockSpec(memory_space=pl.ANY),
-                  pl.BlockSpec(memory_space=pltpu.VMEM), pl.BlockSpec(memory_space=pl.ANY)],
-        out_specs=[pl.BlockSpec(memory_space=pltpu.VMEM)] * 2,
+        in_specs=[pl.BlockSpec(memory_space=pl.ANY)] * 4,
+        out_specs=[pl.BlockSpec(memory_space=pl.ANY), pl.BlockSpec(memory_space=vm)],
         scratch_shapes=[vm((sc, lb, bs, bs), bf16)]
         + [vm((ext, hw, bs), bf16)] * (FILTER * HALVES)
         + [vm((groups * HALO, hw, bs), bf16)] * (FILTER * HALVES)
         + [vm((lb, hw, bs), f32)] * ((FILTER - 1) * HALVES)
         + [vm((lb, hw, bs), bf16)] * HALVES
+        + [vm((parts * HALVES, lb, hw, bs), bf16), vm((lb, 1, bs), f32), vm(cols.shape[::-1], jnp.int32),
+           vm((8, 128), jnp.int32), vm((24 + 2 * sc, 128), jnp.int32),
+           pltpu.SMEM((8, 128), jnp.int32), pltpu.SMEM((24 + 2 * sc, 128), jnp.int32)]
         + [vm((width, full), f32), vm((rps, full), f32), vm((rows, rps, full), f32)]
         + [dma((lb // UNROLL,)), dma((HALVES, lb)), dma((HALVES, lb)),
            dma((FILTER, HALVES, groups)), dma((FILTER, HALVES, groups)),
            dma((hops, HALVES, lb // UNROLL)), dma((hops, HALVES, lb // UNROLL)),
-           dma((rows,)), dma((rows,)), dma((everyone,)), dma((everyone,))],
+           dma((rows,)), dma((rows,)), dma((everyone,)), dma((everyone,)), dma((4,)), dma],
         compiler_params=pltpu.CompilerParams(
             collective_id=0, has_side_effects=True, vmem_limit_bytes=56 * 1024 * 1024),
         name="filter",
-    )(tab, subspace, onsite.reshape(lb, 1, bs), blocks)
+    )(cols.T, subspace, onsite.reshape(lb, 1, bs), blocks)
 
 
 def eliminate(src, up, low):

time: 80.7 us -> 74.6 us (0.924)
  local copies, waits for them, and re-layouts: 2.7 us -> 0 us
  Pallas kernels: 75.6 us -> 73.6 us
  other arithmetic: 1.26 us -> 0 us
    pallas_call x1, Pallas kernels: 63.4 us -> 61.4 us  [filtered(): pl.pallas_call(functools.partial(filter_kernel, rows, parts, lb, sc), out...]
    dynamic_slice x6 -> x0, local copies, waits for them, and re-layouts: 1.33 us -> none  [the longest x2 0.99 us: index_tables(): own = lax.dynamic_slice_in_dim(cols, me * lb, lb, 0).reshape(-1)]
where the time goes in v2:
time: 74.6 us; the launch traced here: 74.4 us
  Pallas kernels  73.6 us (99%)
  between operations  0.8 us (1%)
    pallas_call x1, Pallas kernels, filtered(): pl.pallas_call(functools.partial(filter_kernel, rows, parts, lb, sc), out...  61.4 us
    pallas_call x1, Pallas kernels, body(): pl.pallas_call(functools.partial(finish_kernel, root), out_shape=(jax.Sha...  12.2 us

profile of v2, /device:TPU:0, one launch (start us, length us, event | category | flops | bytes accessed | tf_op | source)
XLA Modules:
  0.0 74.4 jit_solution(15756041208699465948)
XLA Ops:
  0.6 61.4 %filter.1 = (bf16[4,32,64,128]{3,2,1,0:T(8,128)(2,1)}, f32[256,256]{1,0:T(8,128)}) custom-call(s32[20,256]{1,0:T(8,128)} %bitcast.3, bf16[64,4096]{1,0:T(8,128)(2,1)} %sub.1, f32[32,1,128]{2,1,0:T(1,128)} %bitcast.4, bf16[20,32,128,128]{3,2,1,0:T(8,128)(2,1)} %blk.1), custom_call_target="tpu_custom_call" | custom-call | tf_op jit(solution)/shard_map/filter/pallas_call | solution.py:517
  62.1 12.2 %finish.1 = (f32[64,4096]{1,0:T(8,128)}, f32[256,256]{1,0:T(8,128)}) custom-call(s32[1]{0:T(128)} %bitcast.col, bf16[4,32,64,128]{3,2,1,0:T(8,128)(2,1)} %get-tuple-element.4.stored, f32[256,256]{1,0:T(8,128)} %get-tuple-element.5.gram), custom_call_target="tpu_custom_call" | custom-call | tf_op jit(solution)/shard_map/finish/pallas_call | solution.py:630

commit v3 on v2

--- a/solution.py
+++ b/solution.py
@@ -122,7 +122,8 @@
     return max(8, width // rows)
 
 
-def filter_kernel(rows, parts, lb, sc, cols, sub, ons_in, blk, stored, gram, bm, *refs):
+def filter_kernel(rows, parts, lb, sc, cols, sub, ons_in, blk, stored, gram, first_up,
+                  first_low, bm, *refs):
     refs = list(refs)
     take = lambda n: [refs.pop(0) for _ in range(n)]
     halves = range(HALVES)
@@ -186,6 +187,49 @@
     early_v[...] = packed_exports(masks, lb, lane)
     to_early = pltpu.make_async_copy(early_v, early, tsem.at[2])
     to_early.start()
+
+    to_late = pltpu.make_async_copy(late_v, late, tsem.at[3])
+    shift = lax.rem(me, 128 // lb) * lb
+    pn, pp, span = 24, 24 + sc, xs[0][0].shape[0]
+
+    def export(k, g, m):
+        return byte_of(early[groups + g, 0] if k == 0 else late[groups + g, 0], m, lb)
+
+    def permuted(j):
+        return byte_of(late[8 + lax.rem(j, 8), 0], j // 8, lb)
+
+    def offset_of(g):
+        if isinstance(g, int):
+            return shifts[g]
+        found = shifts[-1]
+        for n in range(groups - 1):
+            found = jnp.where(g == n, shifts[n], found)
+        return found
+
+    def copy(k, h, g):
+        return pltpu.make_async_remote_copy(
+            src_ref=snds[k][h].at[pl.ds(g * HALO, HALO)],
+            dst_ref=xs[k][h].at[pl.ds(lb + g * HALO, HALO)],
+            send_sem=ssem.at[k, h, g], recv_sem=rsem.at[k, h, g],
+            device_id=(lax.rem(me - offset_of(g) + rows, rows), mc),
+            device_id_type=pl.DeviceIdType.MESH)
+
+    def pack(k, h, g, source):
+        for m in range(HALO):
+            snds[k][h][g * HALO + m] = source[export(k, g, m)].astype(bf16)
+
+    for h in halves:
+        @pl.loop(0, lb)
+        def _(i):
+            first(i, h)[1].wait()
+
+        to_early.wait()
+        for g in range(groups):
+            pack(0, h, g, s0[h])
+        if h == 0:
+            pl.semaphore_wait(barrier, everyone - 1)
+        for g in range(groups):
+            copy(0, h, g).start()
 
     inverse = order_of(masks, groups, jnp.minimum(lane, lb - 1))
     late_v[0:8, :] = packed_exports(masks, lb, inverse)
@@ -210,41 +254,6 @@
                             lb + HALO * g + ones_in(mask_row(masks, g) & bits_below(at)), far)
         late_v[24 + o:32 + o, :] = jnp.where(near, low, far)
         late_v[24 + sc + o:32 + sc + o, :] = jnp.where(near, order_of(masks, groups, low), far)
-    to_late = pltpu.make_async_copy(late_v, late, tsem.at[3])
-    shift = lax.rem(me, per) * lb
-    pn, pp, span = 24, 24 + sc, xs[0][0].shape[0]
-
-    def export(k, g, m):
-        return byte_of(early[groups + g, 0] if k == 0 else late[groups + g, 0], m, lb)
-
-    def permuted(j):
-        return byte_of(late[8 + lax.rem(j, 8), 0], j // 8, lb)
-
-    def copy(k, h, g):
-        return pltpu.make_async_remote_copy(
-            src_ref=snds[k][h].at[pl.ds(g * HALO, HALO)],
-            dst_ref=xs[k][h].at[pl.ds(lb + g * HALO, HALO)],
-            send_sem=ssem.at[k, h, g], recv_sem=rsem.at[k, h, g],
-            device_id=(lax.rem(me - shifts[g] + rows, rows), mc),
-            device_id_type=pl.DeviceIdType.MESH)
-
-    def pack(k, h, g, source):
-        for m in range(HALO):
-            snds[k][h][g * HALO + m] = source[export(k, g, m)].astype(bf16)
-
-    for h in halves:
-        @pl.loop(0, lb)
-        def _(i):
-            first(i, h)[1].wait()
-
-        to_early.wait()
-        for g in range(groups):
-            pack(0, h, g, s0[h])
-        if h == 0:
-            pl.semaphore_wait(barrier, everyone - 1)
-        for g in range(groups):
-            copy(0, h, g).start()
-
     to_late.start()
     for h in halves:
         @pl.loop(0, lb)
@@ -326,38 +335,42 @@
         for k in range(FILTER):
             for g in range(groups):
                 copy(k, 0, g).wait_recv()
-            ahead = groups if k < FILTER - 1 else 0
-            for c in range(0, ahead, 2):
-                for q in range(2):
-                    feed(k, rows_of(k, c + q), sets[q])
-                if c:
-                    copy(k + 1, 0, c - 1).start()
-                for q in range(2):
-                    chunk(k, c + q, sets[q])
-                    if q:
-                        copy(k + 1, 0, c).start()
-                    pack(k + 1, 0, c + q, ys[k][0])
-
-            @pl.loop(ahead // 2, chunks // 2)
-            def _(cc):
+            last = k == FILTER - 1
+            ahead = 0 if last else groups
+
+            def eight(cc, send):
                 for q in range(2):
                     feed(k, rows_of(k, 2 * cc + q), sets[q])
-                if ahead:
+                if last:
+                    @pl.when(cc > 0)
+                    def _():
+                        for n in firsts:
+                            spread(n, 0, 2 * cc - 1).start()
+                elif send:
+                    @pl.when(cc > 0)
+                    def _():
+                        copy(k + 1, 0, 2 * cc - 1).start()
+                else:
                     @pl.when(cc == ahead // 2)
                     def _():
                         copy(k + 1, 0, ahead - 1).start()
-                for q in range(2):
-                    chunk(k, 2 * cc + q, sets[q])
-                if k == FILTER - 1:
-                    @pl.when(cc > 0)
-                    def _():
-                        for n in firsts:
-                            for q in range(2):
-                                spread(n, 0, 2 * cc - 2 + q).start()
-            if k == FILTER - 1:
+                chunk(k, 2 * cc, sets[0])
+                if send:
+                    pack(k + 1, 0, 2 * cc, ys[k][0])
+                chunk(k, 2 * cc + 1, sets[1])
+                if send:
+                    copy(k + 1, 0, 2 * cc).start()
+                    pack(k + 1, 0, 2 * cc + 1, ys[k][0])
+                if last:
+                    for n in firsts:
+                        spread(n, 0, 2 * cc).start()
+
+            if ahead:
+                pl.loop(0, ahead // 2)(functools.partial(eight, send=True))
+            pl.loop(ahead // 2, chunks // 2)(functools.partial(eight, send=False))
+            if last:
                 for n in firsts:
-                    for q in range(2):
-                        spread(n, 0, chunks - 2 + q).start()
+                    spread(n, 0, chunks - 1).start()
 
     pl.run_scoped(filtering, *[pltpu.ACC(m)((width, 2 * bs), f32)
                                for _ in range(2) for m in range(2) for _ in range(2)])
@@ -391,61 +404,48 @@
     leaves = [n for n in range(len(hops)) if n not in needs.values()]
     near = [n for n in leaves if sum(hops[n]) < top]
     other = [n for n in leaves if sum(hops[n]) >= top]
-    relay(0, chunks // 2)
-    arrive(0, chunks, near)
-    arrive(0, chunks // 2, other)
-
     side = mc // top
     half = lb // 2
+    across = top * width
 
     def tall(q, first_row):
         return jnp.concatenate([out[q, first_row], out[q, first_row + 1]], axis=1)
 
-    def gramming(*accs):
-        both, one, two = [accs[2 * n:2 * n + 2] for n in range(3)]
-
-        @pl.loop(0, half // 4)
+    def gram_part(phase, where, start, count, *accs):
+        one, two = accs[:2], accs[2:]
+
+        @pl.loop(0, count // 8)
         def _(c):
             for m in range(2):
-                row = side * half + c * 4 + 2 * m
+                row = start + c * 8 + 4 * m
                 pltpu.matmul_push_rhs(
-                    jnp.concatenate([tall(q, row) for q in range(parts)], axis=0),
-                    0, m, transpose=True)
-                pltpu.matmul_acc_lhs(both[m], tall(mc, row), load_staged_rhs=0)
-
-        @pl.loop(0, half // 8)
-        def _(c):
-            for m in range(2):
-                row = (1 - side) * half + c * 8 + 4 * m
-                pltpu.matmul_push_rhs(
-                    jnp.concatenate([tall(side * top + q, row + r)
+                    jnp.concatenate([tall(where * top + q, row + r)
                                      for r in (0, 2) for q in range(top)], axis=0),
                     0, m, transpose=True)
                 pltpu.matmul_acc_lhs(one[m], tall(mc, row), load_staged_rhs=0)
                 pltpu.matmul_acc_lhs(two[m], tall(mc, row + 2))
 
-        across = top * width
-        gp[...] = pltpu.matmul_pop(both[0]) + pltpu.matmul_pop(both[1])
-        cut = pl.ds(pl.multiple_of(side * across, across), across)
-        near_sum = [pltpu.matmul_pop(one[m])[:, :across] + pltpu.matmul_pop(two[m])[:, across:]
-                    for m in range(2)]
-        gp[:, cut] += near_sum[0] + near_sum[1]
-
-    pl.run_scoped(gramming, *[pltpu.ACC(m)((width, parts * width), f32)
-                              for _ in range(3) for m in range(2)])
-
-    def part_to(d):
+        sums = [pltpu.matmul_pop(one[m])[:, :across] + pltpu.matmul_pop(two[m])[:, across:]
+                for m in range(2)]
+        gp[phase] = sums[0] + sums[1]
+
+    def grams(phase, *where):
+        pl.run_scoped(functools.partial(gram_part, phase, *where),
+                      *[pltpu.ACC(m)((width, 2 * across), f32) for _ in range(2) for m in range(2)])
+
+    def part_to(phase, d):
         to = lax.rem(me + d, rows)
         lo = pl.multiple_of(to * rps, rps)
         return to, pltpu.make_async_remote_copy(
-            src_ref=gp.at[pl.ds(lo, rps)], dst_ref=rb.at[d], send_sem=pss.at[d],
-            recv_sem=prs.at[d], device_id=(to, mc), device_id_type=pl.DeviceIdType.MESH)
-
-    def part_in(d):
+            src_ref=gp.at[phase, pl.ds(lo, rps)], dst_ref=rb.at[phase, d],
+            send_sem=pss.at[phase, d], recv_sem=prs.at[phase, d], device_id=(to, mc),
+            device_id_type=pl.DeviceIdType.MESH)
+
+    def part_in(phase, d):
         return pltpu.make_async_remote_copy(
-            src_ref=gp.at[pl.ds(0, rps)], dst_ref=rb.at[d], send_sem=pss.at[d],
-            recv_sem=prs.at[d], device_id=(lax.rem(me + 1, rows), mc),
-            device_id_type=pl.DeviceIdType.MESH)
+            src_ref=gp.at[phase, pl.ds(0, rps)], dst_ref=rb.at[phase, d],
+            send_sem=pss.at[phase, d], recv_sem=prs.at[phase, d],
+            device_id=(lax.rem(me + 1, rows), mc), device_id_type=pl.DeviceIdType.MESH)
 
     def only(cond, run):
         if reducers == rows:
@@ -453,53 +453,76 @@
         else:
             pl.when(cond)(run)
 
-    @pl.loop(1, rows)
-    def _(d):
-        to, c = part_to(d)
-        only(to < reducers, lambda: c.start())
-
-    def all_to(e, sender):
+    def scatter(phase):
+        @pl.loop(1, rows)
+        def _(d):
+            to, c = part_to(phase, d)
+            only(to < reducers, lambda: c.start())
+
+    def spot(phase, sender):
+        part = lax.rem(sender, parts)
+        block = part // top if phase == 0 else 1 - part // top
+        lo = pl.multiple_of((part * reducers + sender // parts) * rps, rps)
+        return pl.ds(lo, rps), pl.ds(pl.multiple_of(block * across, across), across)
+
+    def all_to(phase, e, sender):
         to = lax.rem(linear + e, everyone)
-        lo = pl.multiple_of((lax.rem(sender, parts) * reducers + sender // parts) * rps, rps)
         return pltpu.make_async_remote_copy(
-            src_ref=gs, dst_ref=gram.at[pl.ds(lo, rps)], send_sem=ass.at[e],
-            recv_sem=ars.at[e], device_id=(to // parts, lax.rem(to, parts)),
+            src_ref=gs.at[phase], dst_ref=gram.at[spot(phase, sender)], send_sem=ass.at[phase, e],
+            recv_sem=ars.at[phase, e], device_id=(to // parts, lax.rem(to, parts)),
             device_id_type=pl.DeviceIdType.MESH)
 
-    def reduce():
+    def reduce(phase):
         lo = pl.multiple_of(me * rps, rps)
-        total = gp[pl.ds(lo, rps)]
+        total = gp[phase, pl.ds(lo, rps)]
         for d in range(1, rows):
-            part_in(d).wait_recv()
-            total = total + rb[d]
-        gs[...] = total
-        gram[pl.ds(pl.multiple_of((mc * reducers + me) * rps, rps), rps)] = total
+            part_in(phase, d).wait_recv()
+            total = total + rb[phase, d]
+        gs[phase] = total
+        gram[spot(phase, linear)] = total
 
         @pl.loop(1, everyone)
         def _(e):
-            all_to(e, linear).start()
-
-    only(me < reducers, reduce)
+            all_to(phase, e, linear).start()
+
+    def gathered(phase):
+        @pl.loop(1, everyone)
+        def _(e):
+            sender = lax.rem(linear - e + everyone, everyone)
+            only(sender // parts < reducers, lambda: all_to(phase, e, sender).wait_recv())
+
+    arrive(0, chunks, near)
+    grams(0, side, 0, lb)
+    scatter(0)
+    relay(0, chunks // 2)
+    arrive(0, chunks // 2, other)
+    grams(1, 1 - side, side * half, half)
+    scatter(1)
+    only(me < reducers, functools.partial(reduce, 0))
+    only(me < reducers, functools.partial(reduce, 1))
     relay(chunks // 2, chunks)
+    gathered(0)
+    eliminate([gram[8 * t:8 * t + 8, :across] for t in range(across // 8)], first_up, first_low)
     arrive(chunks // 2, chunks, other)
     keep_all = pltpu.make_async_copy(out, stored, osem)
     keep_all.start()
+    gathered(1)
     for h in halves:
         @pl.loop(0, chunks)
         def _(c):
             for n in range(len(hops)):
                 spread(n, h, c).wait_send()
 
-    @pl.loop(1, rows)
-    def _(d):
-        to, c = part_to(d)
-        only(to < reducers, lambda: c.wait_send())
-
-    @pl.loop(1, everyone)
-    def _(e):
-        sender = lax.rem(linear - e + everyone, everyone)
-        only(me < reducers, lambda: all_to(e, linear).wait_send())
-        only(sender // parts < reducers, lambda: all_to(e, sender).wait_recv())
+    for phase in range(2):
+        @pl.loop(1, rows)
+        def _(d):
+            to, c = part_to(phase, d)
+            only(to < reducers, lambda: c.wait_send())
+
+        @pl.loop(1, everyone)
+        def _(e):
+            only(me < reducers, lambda: all_to(phase, e, linear).wait_send())
+
     keep_all.wait()
 
 
@@ -513,13 +536,14 @@
     ext = pl.next_power_of_2(lb + groups * HALO)
     vm, dma = pltpu.VMEM, pltpu.SemaphoreType.DMA
     full, hw = parts * width, width // HALVES
+    half = full // 2
     rps = slice_of(width, rows)
     return pl.pallas_call(
         functools.partial(filter_kernel, rows, parts, lb, sc),
         out_shape=(jax.ShapeDtypeStruct((parts * HALVES, lb, hw, bs), bf16),
-                   jax.ShapeDtypeStruct((full, full), f32)),
+                   jax.ShapeDtypeStruct((full, full), f32)) + (jax.ShapeDtypeStruct((half, half), f32),) * 2,
         in_specs=[pl.BlockSpec(memory_space=pl.ANY)] * 4,
-        out_specs=[pl.BlockSpec(memory_space=pl.ANY), pl.BlockSpec(memory_space=vm)],
+        out_specs=[pl.BlockSpec(memory_space=pl.ANY)] + [pl.BlockSpec(memory_space=vm)] * 3,
         scratch_shapes=[vm((sc, lb, bs, bs), bf16)]
         + [vm((ext, hw, bs), bf16)] * (FILTER * HALVES)
         + [vm((groups * HALO, hw, bs), bf16)] * (FILTER * HALVES)
@@ -528,21 +552,20 @@
         + [vm((parts * HALVES, lb, hw, bs), bf16), vm((lb, 1, bs), f32), vm(cols.shape[::-1], jnp.int32),
            vm((8, 128), jnp.int32), vm((24 + 2 * sc, 128), jnp.int32),
            pltpu.SMEM((8, 128), jnp.int32), pltpu.SMEM((24 + 2 * sc, 128), jnp.int32)]
-        + [vm((width, full), f32), vm((rps, full), f32), vm((rows, rps, full), f32)]
+        + [vm((2, width, half), f32), vm((2, rps, half), f32), vm((2, rows, rps, half), f32)]
         + [dma((lb // UNROLL,)), dma((HALVES, lb)), dma((HALVES, lb)),
            dma((FILTER, HALVES, groups)), dma((FILTER, HALVES, groups)),
            dma((hops, HALVES, lb // UNROLL)), dma((hops, HALVES, lb // UNROLL)),
-           dma((rows,)), dma((rows,)), dma((everyone,)), dma((everyone,)), dma((4,)), dma],
+           dma((2, rows)), dma((2, rows)), dma((2, everyone)), dma((2, everyone)), dma((4,)), dma],
         compiler_params=pltpu.CompilerParams(
             collective_id=0, has_side_effects=True, vmem_limit_bytes=56 * 1024 * 1024),
         name="filter",
     )(cols.T, subspace, onsite.reshape(lb, 1, bs), blocks)
 
 
-def eliminate(src, up, low):
-    n = src.shape[0]
-    tiles = n // 8
-    a = [src[8 * t:8 * t + 8, :] for t in range(tiles)]
+def eliminate(a, up, low):
+    tiles = len(a)
+    n = 8 * tiles
     sub = lax.broadcasted_iota(jnp.int32, (8, n), 0)
     lane = lax.broadcasted_iota(jnp.int32, (8, n), 1)
     b = [jnp.where(lane == sub + 8 * t, 1.0, 0.0).astype(f32) for t in range(tiles)]
@@ -573,7 +596,7 @@
         low[8 * p:8 * p + 8, :] = b[p] * scale
 
 
-def finish_kernel(root, col, stored, gram, basis, factor, work, up, low, inv, whole, sem):
+def finish_kernel(root, col, stored, gram, first_up, first_low, basis, factor, up, low, inv, whole, sem):
     fetch = pltpu.make_async_copy(stored, whole, sem)
     fetch.start()
     parts, lb, _, bs = whole.shape
@@ -582,28 +605,19 @@
     half = full // 2
     exact = functools.partial(lax.dot_general, precision=lax.Precision.HIGHEST,
                               preferred_element_type=f32)
-    nn, nt, tn = ((((1,), (0,)), ((), ())), (((1,), (1,)), ((), ())), (((0,), (0,)), ((), ())))
+    nn, tn = (((1,), (0,)), ((), ())), (((0,), (0,)), ((), ()))
     corner = gram[:half, half:] + gram[half:, :half].T
-    work[...] = gram[:half, :half]
+    across = exact(first_low[...], corner, nn)
+    rest = gram[half:, half:] - exact(across, across, tn)
+    eliminate([rest[8 * t:8 * t + 8, :] for t in range(half // 8)], up, low)
     factor[half:, :half] = jnp.zeros((half, half), f32)
     inv[:half, half:] = jnp.zeros((half, half), f32)
-
-    @pl.loop(0, 2)
-    def _(i):
-        eliminate(work, up.at[i], low.at[i])
-
-        @pl.when(i == 0)
-        def _():
-            across = exact(low[0], corner, nn)
-            factor[:half, half:] = across * (1.0 / root)
-            work[...] = gram[half:, half:] - exact(across, across, tn)
-
-    across = factor[:half, half:] * root
-    inv[:half, :half] = low[0]
-    inv[half:, half:] = low[1]
-    inv[half:, :half] = -exact(low[1], exact(across, low[0], tn), nn)
-    factor[:half, :half] = up[0] * (1.0 / root)
-    factor[half:, half:] = up[1] * (1.0 / root)
+    inv[:half, :half] = first_low[...]
+    inv[half:, half:] = low[...]
+    inv[half:, :half] = -exact(low[...], exact(across, first_low[...], tn), nn)
+    factor[:half, :half] = first_up[...] * (1.0 / root)
+    factor[:half, half:] = across * (1.0 / root)
+    factor[half:, half:] = up[...] * (1.0 / root)
 
     mine = inv[pl.ds(pl.multiple_of(col[0] * width, width), width), :] * root
     high = mine.astype(bf16)
@@ -622,7 +636,7 @@
 def body(subspace, onsite, blocks, cols):
     row_count = lax.axis_size("row")
     part_width, local_rows = subspace.shape
-    whole, gram = filtered(subspace, onsite, blocks, cols)
+    whole, gram, first_up, first_low = filtered(subspace, onsite, blocks, cols)
     full = gram.shape[0]
     half = full // 2
     root = math.sqrt(row_count * local_rows)
@@ -632,13 +646,12 @@
         out_shape=(jax.ShapeDtypeStruct((part_width, local_rows), f32),
                    jax.ShapeDtypeStruct((full, full), f32)),
         in_specs=[pl.BlockSpec(memory_space=pltpu.SMEM), pl.BlockSpec(memory_space=pltpu.HBM),
-                  pl.BlockSpec(memory_space=vm)],
+                  *[pl.BlockSpec(memory_space=vm)] * 3],
         out_specs=[pl.BlockSpec(memory_space=vm)] * 2,
-        scratch_shapes=[vm((half, half), f32), vm((2, half, half), f32), vm((2, half, half), f32),
-                        vm((full, full), f32), vm(whole.shape, bf16), pltpu.SemaphoreType.DMA],
+        scratch_shapes=[vm((half, half), f32), vm((half, half), f32), vm((full, full), f32), vm(whole.shape, bf16), pltpu.SemaphoreType.DMA],
         compiler_params=pltpu.CompilerParams(vmem_limit_bytes=60 * 1024 * 1024),
         name="finish",
-    )(lax.axis_index("col").astype(jnp.int32).reshape(1), whole, gram)
+    )(lax.axis_index("col").astype(jnp.int32).reshape(1), whole, gram, first_up, first_low)
 
 
 def solution(mesh):

time: 74.6 us -> 72.6 us (0.973)
  Pallas kernels: 73.6 us -> 71.6 us
    pallas_call x1, Pallas kernels: 12.2 us -> 8.82 us  [body(): pl.pallas_call(functools.partial(finish_kernel, root), out_shape=(jax.Sha...]
    pallas_call x1, Pallas kernels: 61.4 us -> 62.8 us  [filtered(): pl.pallas_call(functools.partial(filter_kernel, rows, parts, lb, sc), out...]
where the time goes in v3:
time: 72.6 us; the launch traced here: 72.4 us
  Pallas kernels  71.6 us (99%)
  between operations  0.8 us (1%)
    pallas_call x1, Pallas kernels, filtered(): pl.pallas_call(functools.partial(filter_kernel, rows, parts, lb, sc), out...  62.8 us
    pallas_call x1, Pallas kernels, body(): pl.pallas_call(functools.partial(finish_kernel, root), out_shape=(jax.Sha...  8.82 us

profile of v3, /device:TPU:0, one launch (start us, length us, event | category | flops | bytes accessed | tf_op | source)
XLA Modules:
  0.0 72.4 jit_solution(12047280679972790109)
XLA Ops:
  0.6 62.8 %filter.1 = (bf16[4,32,64,128]{3,2,1,0:T(8,128)(2,1)}, f32[256,256]{1,0:T(8,128)}, f32[128,128]{1,0:T(8,128)}, f32[128,128]{1,0:T(8,128)}) custom-call(s32[20,256]{1,0:T(8,128)} %bitcast.3, bf16[64,4096]{1,0:T(8,128)(2,1)} %sub.1, f32[32,1,128]{2,1,0:T(1,128)} %bitcast.4, bf16[20,32,128,128]{3,2,1,0:T(8,128)(2,1)} %blk.1), custom_call_target="tpu_custom_call" | custom-call | tf_op jit(solution)/shard_map/filter/pallas_call | solution.py:541
  63.4 8.8 %finish.1 = (f32[64,4096]{1,0:T(8,128)}, f32[256,256]{1,0:T(8,128)}) custom-call(s32[1]{0:T(128)} %bitcast.col, bf16[4,32,64,128]{3,2,1,0:T(8,128)(2,1)} %get-tuple-element.6.stored, f32[256,256]{1,0:T(8,128)} %get-tuple-element.7.gram, f32[128,128]{1,0:T(8,128)} %get-tuple-element.8.first_up, f32[128,128]{1,0:T(8,128)} %get-tuple-element.9.first_low), custom_call_target="tpu_custom_call" | custom-call | tf_op jit(solution)/shard_map/finish/pallas_call | solution.py:644

commit v4 on v3

--- a/solution.py
+++ b/solution.py
@@ -156,6 +156,8 @@
         return (pltpu.make_async_copy(cut, xs[0][h].at[i], xsem.at[h, i]),
                 pltpu.make_async_copy(cut, s0[h].at[i], csem.at[h, i]))
 
+    named = pltpu.make_async_copy(cols, cvm, tsem.at[0])
+    named.start()
     barrier = pltpu.get_barrier_semaphore()
 
     @pl.loop(1, everyone)
@@ -164,14 +166,10 @@
         pl.semaphore_signal(barrier, inc=1, device_id=(to // parts, lax.rem(to, parts)),
                             device_id_type=pl.DeviceIdType.MESH)
 
-    named = pltpu.make_async_copy(cols, cvm, tsem.at[0])
-    named.start()
     for h in halves:
         @pl.loop(0, lb)
         def _(i):
-            a, b = first(i, h)
-            b.start()
-            a.start()
+            first(i, h)[1].start()
 
     energies = pltpu.make_async_copy(ons_in, ons, tsem.at[1])
     energies.start()
@@ -230,6 +228,11 @@
             pl.semaphore_wait(barrier, everyone - 1)
         for g in range(groups):
             copy(0, h, g).start()
+
+    for h in halves:
+        @pl.loop(0, lb)
+        def _(i):
+            first(i, h)[0].start()
 
     inverse = order_of(masks, groups, jnp.minimum(lane, lb - 1))
     late_v[0:8, :] = packed_exports(masks, lb, inverse)
@@ -336,41 +339,29 @@
             for g in range(groups):
                 copy(k, 0, g).wait_recv()
             last = k == FILTER - 1
-            ahead = 0 if last else groups
-
-            def eight(cc, send):
+
+            def sent(c):
+                if last:
+                    for n in firsts:
+                        spread(n, 0, c).start()
+
+            @pl.loop(0, groups)
+            def _(c):
+                feed(k, rows_of(k, c), sets[0])
+                chunk(k, c, sets[0])
+                if not last:
+                    pack(k + 1, 0, c, ys[k][0])
+                    copy(k + 1, 0, c).start()
+                sent(c)
+
+            @pl.loop(groups // 2, chunks // 2)
+            def _(cc):
                 for q in range(2):
                     feed(k, rows_of(k, 2 * cc + q), sets[q])
-                if last:
-                    @pl.when(cc > 0)
-                    def _():
-                        for n in firsts:
-                            spread(n, 0, 2 * cc - 1).start()
-                elif send:
-                    @pl.when(cc > 0)
-                    def _():
-                        copy(k + 1, 0, 2 * cc - 1).start()
-                else:
-                    @pl.when(cc == ahead // 2)
-                    def _():
-                        copy(k + 1, 0, ahead - 1).start()
-                chunk(k, 2 * cc, sets[0])
-                if send:
-                    pack(k + 1, 0, 2 * cc, ys[k][0])
-                chunk(k, 2 * cc + 1, sets[1])
-                if send:
-                    copy(k + 1, 0, 2 * cc).start()
-                    pack(k + 1, 0, 2 * cc + 1, ys[k][0])
-                if last:
-                    for n in firsts:
-                        spread(n, 0, 2 * cc).start()
-
-            if ahead:
-                pl.loop(0, ahead // 2)(functools.partial(eight, send=True))
-            pl.loop(ahead // 2, chunks // 2)(functools.partial(eight, send=False))
-            if last:
-                for n in firsts:
-                    spread(n, 0, chunks - 1).start()
+                for q in range(2):
+                    chunk(k, 2 * cc + q, sets[q])
+                for q in range(2):
+                    sent(2 * cc + q)
 
     pl.run_scoped(filtering, *[pltpu.ACC(m)((width, 2 * bs), f32)
                                for _ in range(2) for m in range(2) for _ in range(2)])
@@ -502,10 +493,10 @@
     only(me < reducers, functools.partial(reduce, 1))
     relay(chunks // 2, chunks)
     gathered(0)
-    eliminate([gram[8 * t:8 * t + 8, :across] for t in range(across // 8)], first_up, first_low)
     arrive(chunks // 2, chunks, other)
     keep_all = pltpu.make_async_copy(out, stored, osem)
     keep_all.start()
+    eliminate([gram[8 * t:8 * t + 8, :across] for t in range(across // 8)], first_up, first_low)
     gathered(1)
     for h in halves:
         @pl.loop(0, chunks)
@@ -596,8 +587,13 @@
         low[8 * p:8 * p + 8, :] = b[p] * scale
 
 
-def finish_kernel(root, col, stored, gram, first_up, first_low, basis, factor, up, low, inv, whole, sem):
-    fetch = pltpu.make_async_copy(stored, whole, sem)
+def finish_kernel(root, col, stored, gram_in, up_in, low_in, basis_out, factor_out,
+                  basis, factor, up, low, inv, gram, first_up, first_low, whole, sem):
+    operands = [pltpu.make_async_copy(*pair, sem.at[6 + n]) for n, pair in enumerate(
+        ((low_in, first_low), (gram_in, gram), (up_in, first_up)))]
+    for operand in operands:
+        operand.start()
+    fetch = pltpu.make_async_copy(stored, whole, sem.at[0])
     fetch.start()
     parts, lb, _, bs = whole.shape
     width = basis.shape[0]
@@ -606,6 +602,8 @@
     exact = functools.partial(lax.dot_general, precision=lax.Precision.HIGHEST,
                               preferred_element_type=f32)
     nn, tn = (((1,), (0,)), ((), ())), (((0,), (0,)), ((), ()))
+    operands[0].wait()
+    operands[1].wait()
     corner = gram[:half, half:] + gram[half:, :half].T
     across = exact(first_low[...], corner, nn)
     rest = gram[half:, half:] - exact(across, across, tn)
@@ -615,9 +613,12 @@
     inv[:half, :half] = first_low[...]
     inv[half:, half:] = low[...]
     inv[half:, :half] = -exact(low[...], exact(across, first_low[...], tn), nn)
+    operands[2].wait()
     factor[:half, :half] = first_up[...] * (1.0 / root)
     factor[:half, half:] = across * (1.0 / root)
     factor[half:, half:] = up[...] * (1.0 / root)
+    put = [pltpu.make_async_copy(factor, factor_out, sem.at[1])]
+    put[0].start()
 
     mine = inv[pl.ds(pl.multiple_of(col[0] * width, width), width), :] * root
     high = mine.astype(bf16)
@@ -627,10 +628,18 @@
     left = jnp.concatenate([high, mid, last], axis=0)
 
     fetch.wait()
+    every = lb // 4
     for k in range(lb):
         right = jnp.concatenate([whole[q, k] for q in range(parts)], axis=0)
         r = jnp.dot(left, right, preferred_element_type=f32)
         basis[:, k * bs:(k + 1) * bs] = r[:width] + (r[width:2 * width] + r[2 * width:])
+        if k % every == every - 1:
+            cut = pl.ds((k + 1 - every) * bs, every * bs)
+            put.append(pltpu.make_async_copy(basis.at[:, cut], basis_out.at[:, cut],
+                                             sem.at[2 + k // every]))
+            put[-1].start()
+    for copy in put:
+        copy.wait()
 
 
 def body(subspace, onsite, blocks, cols):
@@ -645,10 +654,12 @@
         functools.partial(finish_kernel, root),
         out_shape=(jax.ShapeDtypeStruct((part_width, local_rows), f32),
                    jax.ShapeDtypeStruct((full, full), f32)),
-        in_specs=[pl.BlockSpec(memory_space=pltpu.SMEM), pl.BlockSpec(memory_space=pltpu.HBM),
-                  *[pl.BlockSpec(memory_space=vm)] * 3],
-        out_specs=[pl.BlockSpec(memory_space=vm)] * 2,
-        scratch_shapes=[vm((half, half), f32), vm((half, half), f32), vm((full, full), f32), vm(whole.shape, bf16), pltpu.SemaphoreType.DMA],
+        in_specs=[pl.BlockSpec(memory_space=pltpu.SMEM), *[pl.BlockSpec(memory_space=pltpu.HBM)] * 4],
+        out_specs=[pl.BlockSpec(memory_space=pl.ANY)] * 2,
+        scratch_shapes=[vm((part_width, local_rows), f32), vm((full, full), f32),
+                        vm((half, half), f32), vm((half, half), f32), vm((full, full), f32),
+                        vm((full, full), f32), vm((half, half), f32), vm((half, half), f32),
+                        vm(whole.shape, bf16), pltpu.SemaphoreType.DMA((9,))],
         compiler_params=pltpu.CompilerParams(vmem_limit_bytes=60 * 1024 * 1024),
         name="finish",
     )(lax.axis_index("col").astype(jnp.int32).reshape(1), whole, gram, first_up, first_low)

time: 72.6 us -> 69.8 us (0.961)
  Pallas kernels: 71.6 us -> 68.8 us
    pallas_call x1, Pallas kernels: 62.8 us -> 61.2 us  [filtered(): pl.pallas_call(functools.partial(filter_kernel, rows, parts, lb, sc), out...]
    pallas_call x1, Pallas kernels: 8.82 us -> 7.65 us  [body(): pl.pallas_call(functools.partial(finish_kernel, root), out_shape=(jax.Sha...]
where the time goes in v4:
time: 69.8 us; the launch traced here: 69.6 us
  Pallas kernels  68.8 us (99%)
  between operations  0.8 us (1%)
    pallas_call x1, Pallas kernels, filtered(): pl.pallas_call(functools.partial(filter_kernel, rows, parts, lb, sc), out...  61.2 us
    pallas_call x1, Pallas kernels, body(): pl.pallas_call(functools.partial(finish_kernel, root), out_shape=(jax.Sha...  7.65 us

profile of v4, /device:TPU:0, one launch (start us, length us, event | category | flops | bytes accessed | tf_op | source)
XLA Modules:
  0.0 69.6 jit_solution(9449376172269111677)
XLA Ops:
  0.6 61.2 %filter.1 = (bf16[4,32,64,128]{3,2,1,0:T(8,128)(2,1)}, f32[256,256]{1,0:T(8,128)}, f32[128,128]{1,0:T(8,128)}, f32[128,128]{1,0:T(8,128)}) custom-call(s32[20,256]{1,0:T(8,128)} %bitcast.3, bf16[64,4096]{1,0:T(8,128)(2,1)} %sub.1, f32[32,1,128]{2,1,0:T(1,128)} %bitcast.4, bf16[20,32,128,128]{3,2,1,0:T(8,128)(2,1)} %blk.1), custom_call_target="tpu_custom_call" | custom-call | tf_op jit(solution)/shard_map/filter/pallas_call | solution.py:532
  61.8 7.6 %finish.1 = (f32[64,4096]{1,0:T(8,128)}, f32[256,256]{1,0:T(8,128)}) custom-call(s32[1]{0:T(128)} %bitcast.col, bf16[4,32,64,128]{3,2,1,0:T(8,128)(2,1)} %get-tuple-element.6.stored, f32[256,256]{1,0:T(8,128)} %get-tuple-element.7.gram_in, f32[128,128]{1,0:T(8,128)} %get-tuple-element.8.up_in, f32[128,128]{1,0:T(8,128)} %get-tuple-element.9.low_in), custom_call_target="tpu_custom_call" | custom-call | tf_op jit(solution)/shard_map/finish/pallas_call | solution.py:653

commit v5 on v4

--- a/solution.py
+++ b/solution.py
@@ -18,7 +18,7 @@
 
 
 def shifts_of(rows):
-    return (rows // 2, 2, 1, -1)
+    return (1, -1, 2, rows // 2)
 
 
 def bits_below(k):
@@ -122,8 +122,8 @@
     return max(8, width // rows)
 
 
-def filter_kernel(rows, parts, lb, sc, cols, sub, ons_in, blk, stored, gram, first_up,
-                  first_low, bm, *refs):
+def filter_kernel(rows, parts, lb, sc, cols, sub, ons_in, blk, stored, gram_out, up_out,
+                  low_out, bm, *refs):
     refs = list(refs)
     take = lambda n: [refs.pop(0) for _ in range(n)]
     halves = range(HALVES)
@@ -132,7 +132,7 @@
     ys = [take(HALVES) for _ in range(FILTER - 1)]
     s0 = take(HALVES)
     (out, ons, cvm, early_v, late_v, early, late, gp, gs, rb, bsem, xsem, csem, ssem, rsem,
-     wss, wrs, pss, prs, ass, ars, tsem, osem) = refs
+     wss, wrs, pss, prs, ass, ars, tsem, osem, gram, first_up, first_low) = refs
     me = lax.axis_index("row")
     mc = lax.axis_index("col")
     everyone = rows * parts
@@ -402,7 +402,7 @@
     def tall(q, first_row):
         return jnp.concatenate([out[q, first_row], out[q, first_row + 1]], axis=1)
 
-    def gram_part(phase, where, start, count, *accs):
+    def gram_part(phase, part, start, count, *accs):
         one, two = accs[:2], accs[2:]
 
         @pl.loop(0, count // 8)
@@ -410,11 +410,11 @@
             for m in range(2):
                 row = start + c * 8 + 4 * m
                 pltpu.matmul_push_rhs(
-                    jnp.concatenate([tall(where * top + q, row + r)
+                    jnp.concatenate([tall(side * top + q, row + r)
                                      for r in (0, 2) for q in range(top)], axis=0),
                     0, m, transpose=True)
-                pltpu.matmul_acc_lhs(one[m], tall(mc, row), load_staged_rhs=0)
-                pltpu.matmul_acc_lhs(two[m], tall(mc, row + 2))
+                pltpu.matmul_acc_lhs(one[m], tall(part, row), load_staged_rhs=0)
+                pltpu.matmul_acc_lhs(two[m], tall(part, row + 2))
 
         sums = [pltpu.matmul_pop(one[m])[:, :across] + pltpu.matmul_pop(two[m])[:, across:]
                 for m in range(2)]
@@ -452,7 +452,9 @@
 
     def spot(phase, sender):
         part = lax.rem(sender, parts)
-        block = part // top if phase == 0 else 1 - part // top
+        block = part // top
+        if phase == 1:
+            part = flip(part, top)
         lo = pl.multiple_of((part * reducers + sender // parts) * rps, rps)
         return pl.ds(lo, rps), pl.ds(pl.multiple_of(block * across, across), across)
 
@@ -483,21 +485,30 @@
             only(sender // parts < reducers, lambda: all_to(phase, e, sender).wait_recv())
 
     arrive(0, chunks, near)
-    grams(0, side, 0, lb)
+    grams(0, mc, 0, lb)
     scatter(0)
     relay(0, chunks // 2)
-    arrive(0, chunks // 2, other)
-    grams(1, 1 - side, side * half, half)
+    grams(1, flip(mc, top), side * half, half)
     scatter(1)
     only(me < reducers, functools.partial(reduce, 0))
     only(me < reducers, functools.partial(reduce, 1))
     relay(chunks // 2, chunks)
     gathered(0)
-    arrive(chunks // 2, chunks, other)
-    keep_all = pltpu.make_async_copy(out, stored, osem)
+    arrive(0, chunks, other)
+    keep_all = pltpu.make_async_copy(out, stored, osem.at[0])
     keep_all.start()
-    eliminate([gram[8 * t:8 * t + 8, :across] for t in range(across // 8)], first_up, first_low)
-    gathered(1)
+    keep_gram = pltpu.make_async_copy(gram, gram_out, osem.at[1])
+
+    def between():
+        gathered(1)
+        keep_gram.start()
+
+    eliminate([gram[8 * t:8 * t + 8, :across] for t in range(across // 8)], first_up, first_low,
+              between)
+    keep_first = [pltpu.make_async_copy(first_up, up_out, osem.at[2]),
+                  pltpu.make_async_copy(first_low, low_out, osem.at[3])]
+    for kept in keep_first:
+        kept.start()
     for h in halves:
         @pl.loop(0, chunks)
         def _(c):
@@ -514,7 +525,8 @@
         def _(e):
             only(me < reducers, lambda: all_to(phase, e, linear).wait_send())
 
-    keep_all.wait()
+    for kept in (keep_all, keep_gram, *keep_first):
+        kept.wait()
 
 
 def filtered(subspace, onsite, blocks, cols):
@@ -534,7 +546,7 @@
         out_shape=(jax.ShapeDtypeStruct((parts * HALVES, lb, hw, bs), bf16),
                    jax.ShapeDtypeStruct((full, full), f32)) + (jax.ShapeDtypeStruct((half, half), f32),) * 2,
         in_specs=[pl.BlockSpec(memory_space=pl.ANY)] * 4,
-        out_specs=[pl.BlockSpec(memory_space=pl.ANY)] + [pl.BlockSpec(memory_space=vm)] * 3,
+        out_specs=[pl.BlockSpec(memory_space=pl.ANY)] * 4,
         scratch_shapes=[vm((sc, lb, bs, bs), bf16)]
         + [vm((ext, hw, bs), bf16)] * (FILTER * HALVES)
         + [vm((groups * HALO, hw, bs), bf16)] * (FILTER * HALVES)
@@ -547,14 +559,15 @@
         + [dma((lb // UNROLL,)), dma((HALVES, lb)), dma((HALVES, lb)),
            dma((FILTER, HALVES, groups)), dma((FILTER, HALVES, groups)),
            dma((hops, HALVES, lb // UNROLL)), dma((hops, HALVES, lb // UNROLL)),
-           dma((2, rows)), dma((2, rows)), dma((2, everyone)), dma((2, everyone)), dma((4,)), dma],
+           dma((2, rows)), dma((2, rows)), dma((2, everyone)), dma((2, everyone)), dma((4,)), dma((4,)),
+           vm((full, full), f32), vm((half, half), f32), vm((half, half), f32)],
         compiler_params=pltpu.CompilerParams(
             collective_id=0, has_side_effects=True, vmem_limit_bytes=56 * 1024 * 1024),
         name="filter",
     )(cols.T, subspace, onsite.reshape(lb, 1, bs), blocks)
 
 
-def eliminate(a, up, low):
+def eliminate(a, up, low, between=None):
     tiles = len(a)
     n = 8 * tiles
     sub = lax.broadcasted_iota(jnp.int32, (8, n), 0)
@@ -565,6 +578,8 @@
         return jnp.broadcast_to(v[q:q + 1, :], (8, n))
 
     for p in range(tiles):
+        if between and p == 3 * tiles // 4:
+            between()
         cols = {t: [jnp.broadcast_to(a[t][:, 8 * p + q:8 * p + q + 1], (8, n)) for q in range(8)]
                 for t in range(p, tiles)}
         pivots = jnp.ones((8, n), f32)
@@ -623,16 +638,14 @@
     mine = inv[pl.ds(pl.multiple_of(col[0] * width, width), width), :] * root
     high = mine.astype(bf16)
     rest = mine - high.astype(f32)
-    mid = rest.astype(bf16)
-    last = (rest - mid.astype(f32)).astype(bf16)
-    left = jnp.concatenate([high, mid, last], axis=0)
+    left = jnp.concatenate([high, rest.astype(bf16)], axis=0)
 
     fetch.wait()
     every = lb // 4
     for k in range(lb):
         right = jnp.concatenate([whole[q, k] for q in range(parts)], axis=0)
         r = jnp.dot(left, right, preferred_element_type=f32)
-        basis[:, k * bs:(k + 1) * bs] = r[:width] + (r[width:2 * width] + r[2 * width:])
+        basis[:, k * bs:(k + 1) * bs] = r[:width] + r[width:]
         if k % every == every - 1:
             cut = pl.ds((k + 1 - every) * bs, every * bs)
             put.append(pltpu.make_async_copy(basis.at[:, cut], basis_out.at[:, cut],

time: 69.8 us -> 67.4 us (0.966)
  Pallas kernels: 68.8 us -> 66.5 us
    pallas_call x1, Pallas kernels: 61.2 us -> 59.1 us  [filtered(): pl.pallas_call(functools.partial(filter_kernel, rows, parts, lb, sc), out...]
where the time goes in v5:
time: 67.4 us; the launch traced here: 67.3 us
  Pallas kernels  66.5 us (99%)
  between operations  0.8 us (1%)
    pallas_call x1, Pallas kernels, filtered(): pl.pallas_call(functools.partial(filter_kernel, rows, parts, lb, sc), out...  59.1 us
    pallas_call x1, Pallas kernels, body(): pl.pallas_call(functools.partial(finish_kernel, root), out_shape=(jax.Sha...  7.37 us

profile of v5, /device:TPU:0, one launch (start us, length us, event | category | flops | bytes accessed | tf_op | source)
XLA Modules:
  0.0 67.3 jit_solution(9442451900925797549)
XLA Ops:
  0.6 59.1 %filter.1 = (bf16[4,32,64,128]{3,2,1,0:T(8,128)(2,1)}, f32[256,256]{1,0:T(8,128)}, f32[128,128]{1,0:T(8,128)}, f32[128,128]{1,0:T(8,128)}) custom-call(s32[20,256]{1,0:T(8,128)} %bitcast.3, bf16[64,4096]{1,0:T(8,128)(2,1)} %sub.1, f32[32,1,128]{2,1,0:T(1,128)} %bitcast.4, bf16[20,32,128,128]{3,2,1,0:T(8,128)(2,1)} %blk.1), custom_call_target="tpu_custom_call" | custom-call | tf_op jit(solution)/shard_map/filter/pallas_call | solution.py:544
  59.7 7.4 %finish.1 = (f32[64,4096]{1,0:T(8,128)}, f32[256,256]{1,0:T(8,128)}) custom-call(s32[1]{0:T(128)} %bitcast.col, bf16[4,32,64,128]{3,2,1,0:T(8,128)(2,1)} %get-tuple-element.6.stored, f32[256,256]{1,0:T(8,128)} %get-tuple-element.7.gram_in, f32[128,128]{1,0:T(8,128)} %get-tuple-element.8.up_in, f32[128,128]{1,0:T(8,128)} %get-tuple-element.9.low_in), custom_call_target="tpu_custom_call" | custom-call | tf_op jit(solution)/shard_map/finish/pallas_call | solution.py:666

commit v6 on v5

--- a/solution.py
+++ b/solution.py
@@ -136,7 +136,6 @@
     me = lax.axis_index("row")
     mc = lax.axis_index("col")
     everyone = rows * parts
-    linear = me * parts + mc
     width = sub.shape[0]
     hw = width // HALVES
     hops = hops_of(parts)
@@ -160,11 +159,18 @@
     named.start()
     barrier = pltpu.get_barrier_semaphore()
 
-    @pl.loop(1, everyone)
-    def _(e):
-        to = lax.rem(linear + e, everyone)
-        pl.semaphore_signal(barrier, inc=1, device_id=(to // parts, lax.rem(to, parts)),
-                            device_id_type=pl.DeviceIdType.MESH)
+    def wrapped(x, n):
+        return jnp.where(x >= n, x - n, x)
+
+    part_at = [wrapped(mc + j, parts) for j in range(parts)]
+
+    def greet(d, first_part=0):
+        for j in range(first_part, parts):
+            pl.semaphore_signal(barrier, inc=1, device_id=(wrapped(me + d, rows), part_at[j]),
+                                device_id_type=pl.DeviceIdType.MESH)
+
+    pl.loop(1, rows)(greet)
+    greet(0, 1)
 
     for h in halves:
         @pl.loop(0, lb)
@@ -366,10 +372,6 @@
     pl.run_scoped(filtering, *[pltpu.ACC(m)((width, 2 * bs), f32)
                                for _ in range(2) for m in range(2) for _ in range(2)])
 
-    for k in range(FILTER):
-        for h in halves:
-            for g in range(groups):
-                copy(k, h, g).wait_send()
 
     needs = {n: max(q for q in range(n) if sum(hops[q]) == m)
              for n, (_, m) in enumerate(hops) if m}
@@ -402,13 +404,15 @@
     def tall(q, first_row):
         return jnp.concatenate([out[q, first_row], out[q, first_row + 1]], axis=1)
 
-    def gram_part(phase, part, start, count, *accs):
+    def gram_part(phase, part, row_of, count, ready, *accs):
         one, two = accs[:2], accs[2:]
 
         @pl.loop(0, count // 8)
         def _(c):
+            if ready:
+                ready(c)
             for m in range(2):
-                row = start + c * 8 + 4 * m
+                row = row_of(c) + 4 * m
                 pltpu.matmul_push_rhs(
                     jnp.concatenate([tall(side * top + q, row + r)
                                      for r in (0, 2) for q in range(top)], axis=0),
@@ -450,19 +454,17 @@
             to, c = part_to(phase, d)
             only(to < reducers, lambda: c.start())
 
-    def spot(phase, sender):
-        part = lax.rem(sender, parts)
+    def spot(phase, row, part):
         block = part // top
         if phase == 1:
             part = flip(part, top)
-        lo = pl.multiple_of((part * reducers + sender // parts) * rps, rps)
+        lo = pl.multiple_of((part * reducers + row) * rps, rps)
         return pl.ds(lo, rps), pl.ds(pl.multiple_of(block * across, across), across)
 
-    def all_to(phase, e, sender):
-        to = lax.rem(linear + e, everyone)
+    def all_to(phase, d, j, place):
         return pltpu.make_async_remote_copy(
-            src_ref=gs.at[phase], dst_ref=gram.at[spot(phase, sender)], send_sem=ass.at[phase, e],
-            recv_sem=ars.at[phase, e], device_id=(to // parts, lax.rem(to, parts)),
+            src_ref=gs.at[phase], dst_ref=gram.at[place], send_sem=ass.at[phase, d * parts + j],
+            recv_sem=ars.at[phase, d * parts + j], device_id=(wrapped(me + d, rows), part_at[j]),
             device_id_type=pl.DeviceIdType.MESH)
 
     def reduce(phase):
@@ -472,23 +474,52 @@
             part_in(phase, d).wait_recv()
             total = total + rb[phase, d]
         gs[phase] = total
-        gram[spot(phase, linear)] = total
-
-        @pl.loop(1, everyone)
-        def _(e):
-            all_to(phase, e, linear).start()
+        place = spot(phase, me, mc)
+        gram[place] = total
+
+        def send(d, first_part=0):
+            for j in range(first_part, parts):
+                all_to(phase, d, j, place).start()
+
+        pl.loop(rows // 4, 3 * rows // 4 + 1)(send)
+        pl.loop(3 * rows // 4 + 1, rows)(send)
+        pl.loop(1, rows // 4)(send)
+        send(0, 1)
 
     def gathered(phase):
-        @pl.loop(1, everyone)
-        def _(e):
-            sender = lax.rem(linear - e + everyone, everyone)
-            only(sender // parts < reducers, lambda: all_to(phase, e, sender).wait_recv())
-
-    arrive(0, chunks, near)
-    grams(0, mc, 0, lb)
+        def arrived(d, first_part=0):
+            row = wrapped(me - d + rows, rows)
+
+            def run():
+                for j in range(first_part, parts):
+                    place = spot(phase, row, wrapped(mc - j + parts, parts))
+                    all_to(phase, d, j, place).wait_recv()
+
+            only(row < reducers, run)
+
+        arrived(0, 1)
+        pl.loop(1, rows)(arrived)
+
+    def passed_on(phase):
+        place = spot(phase, me, mc)
+
+        def left(d, first_part=0):
+            for j in range(first_part, parts):
+                all_to(phase, d, j, place).wait_send()
+
+        left(0, 1)
+        pl.loop(1, rows)(left)
+
+
+    def beside(c):
+        for q in range(2):
+            for n in near:
+                spread(n, 0, 2 * c + q).wait_recv()
+
+    grams(0, mc, lambda c: rows_of(FILTER - 1, 2 * c), lb, beside)
     scatter(0)
     relay(0, chunks // 2)
-    grams(1, flip(mc, top), side * half, half)
+    grams(1, flip(mc, top), lambda c: side * half + 8 * c, half, None)
     scatter(1)
     only(me < reducers, functools.partial(reduce, 0))
     only(me < reducers, functools.partial(reduce, 1))
@@ -515,15 +546,18 @@
             for n in range(len(hops)):
                 spread(n, h, c).wait_send()
 
+    for k in range(FILTER):
+        for h in halves:
+            for g in range(groups):
+                copy(k, h, g).wait_send()
+
     for phase in range(2):
         @pl.loop(1, rows)
         def _(d):
             to, c = part_to(phase, d)
             only(to < reducers, lambda: c.wait_send())
 
-        @pl.loop(1, everyone)
-        def _(e):
-            only(me < reducers, lambda: all_to(phase, e, linear).wait_send())
+        only(me < reducers, functools.partial(passed_on, phase))
 
     for kept in (keep_all, keep_gram, *keep_first):
         kept.wait()
@@ -602,7 +636,7 @@
         low[8 * p:8 * p + 8, :] = b[p] * scale
 
 
-def finish_kernel(root, col, stored, gram_in, up_in, low_in, basis_out, factor_out,
+def finish_kernel(root, stored, gram_in, up_in, low_in, basis_out, factor_out,
                   basis, factor, up, low, inv, gram, first_up, first_low, whole, sem):
     operands = [pltpu.make_async_copy(*pair, sem.at[6 + n]) for n, pair in enumerate(
         ((low_in, first_low), (gram_in, gram), (up_in, first_up)))]
@@ -635,7 +669,7 @@
     put = [pltpu.make_async_copy(factor, factor_out, sem.at[1])]
     put[0].start()
 
-    mine = inv[pl.ds(pl.multiple_of(col[0] * width, width), width), :] * root
+    mine = inv[pl.ds(pl.multiple_of(lax.axis_index("col") * width, width), width), :] * root
     high = mine.astype(bf16)
     rest = mine - high.astype(f32)
     left = jnp.concatenate([high, rest.astype(bf16)], axis=0)
@@ -667,7 +701,7 @@
         functools.partial(finish_kernel, root),
         out_shape=(jax.ShapeDtypeStruct((part_width, local_rows), f32),
                    jax.ShapeDtypeStruct((full, full), f32)),
-        in_specs=[pl.BlockSpec(memory_space=pltpu.SMEM), *[pl.BlockSpec(memory_space=pltpu.HBM)] * 4],
+        in_specs=[pl.BlockSpec(memory_space=pltpu.HBM)] * 4,
         out_specs=[pl.BlockSpec(memory_space=pl.ANY)] * 2,
         scratch_shapes=[vm((part_width, local_rows), f32), vm((full, full), f32),
                         vm((half, half), f32), vm((half, half), f32), vm((full, full), f32),
@@ -675,7 +709,7 @@
                         vm(whole.shape, bf16), pltpu.SemaphoreType.DMA((9,))],
         compiler_params=pltpu.CompilerParams(vmem_limit_bytes=60 * 1024 * 1024),
         name="finish",
-    )(lax.axis_index("col").astype(jnp.int32).reshape(1), whole, gram, first_up, first_low)
+    )(whole, gram, first_up, first_low)
 
 
 def solution(mesh):

time: 67.4 us -> 67.6 us (level)
  no operation moved by 1% of the time
where the time goes in v6:
time: 67.6 us; the launch traced here: 67.3 us
  Pallas kernels  66.5 us (98%)
  between operations  0.8 us (1%)
    pallas_call x1, Pallas kernels, filtered(): pl.pallas_call(functools.partial(filter_kernel, rows, parts, lb, sc), out...  59.2 us
    pallas_call x1, Pallas kernels, body(): pl.pallas_call(functools.partial(finish_kernel, root), out_shape=(jax.Sha...  7.37 us

profile of v6, /device:TPU:0, one launch (start us, length us, event | category | flops | bytes accessed | tf_op | source)
XLA Modules:
  0.0 67.3 jit_solution(13333444058579968776)
XLA Ops:
  0.6 59.2 %filter.1 = (bf16[4,32,64,128]{3,2,1,0:T(8,128)(2,1)}, f32[256,256]{1,0:T(8,128)}, f32[128,128]{1,0:T(8,128)}, f32[128,128]{1,0:T(8,128)}) custom-call(s32[20,256]{1,0:T(8,128)} %bitcast.2, bf16[64,4096]{1,0:T(8,128)(2,1)} %sub.1, f32[32,1,128]{2,1,0:T(1,128)} %bitcast.3, bf16[20,32,128,128]{3,2,1,0:T(8,128)(2,1)} %blk.1), custom_call_target="tpu_custom_call" | custom-call | tf_op jit(solution)/shard_map/filter/pallas_call | solution.py:578
  59.8 7.4 %finish.1 = (f32[64,4096]{1,0:T(8,128)}, f32[256,256]{1,0:T(8,128)}) custom-call(bf16[4,32,64,128]{3,2,1,0:T(8,128)(2,1)} %get-tuple-element.6.stored, f32[256,256]{1,0:T(8,128)} %get-tuple-element.7.gram_in, f32[128,128]{1,0:T(8,128)} %get-tuple-element.8.up_in, f32[128,128]{1,0:T(8,128)} %get-tuple-element.9.low_in), custom_call_target="tpu_custom_call" | custom-call | tf_op jit(solution)/shard_map/finish/pallas_call | solution.py:700
